TPU v7x, 1024 devices: a whole 4x8x16 slice. The times are simulated.
1024 devices in a mesh: ctx: 64 (over z, x), ch: 16 (over y, core).
Axes of the slice: x: 4, y: 8, z: 16, core: 2. Of those that a mesh axis runs over, the one named last changes fastest.
Arguments:
- grad_out: bfloat16 [8192, 4096], P('ctx', 'ch'), may hold values from -6 to 6
- out_weight: bfloat16 [4096, 4096], P('ch'), may hold values from -0.09375 to 0.09375
- gate_values: bfloat16 [8192, 4096], P('ctx', 'ch'), may hold values from -6 to 6
- conv_input: bfloat16 [8192, 4096], P('ctx', 'ch'), may hold values from -0.06591797 to 0.06591797
- conv_output: bfloat16 [8192, 4096], P('ctx', 'ch'), may hold values from -6 to 6
- long_filter: float32 [2048, 4096], P('ctx', 'ch'), may hold values from -0.125 to 0.125
- skip_gain: float32 [4096], P('ch'), may hold values from 0.5 to 1.5
Outputs:
- grad_input: bfloat16 [8192, 4096], P('ctx', 'ch')
- grad_gate: bfloat16 [8192, 4096], P('ctx', 'ch')
- grad_filter: float32 [2048, 4096], P('ctx', 'ch')
All inputs are finite; a program needn't handle non-finite values.
Results may differ from a plain program's by a relative error of at most 0.0049.
Values may be sent and summed in bfloat16 or wider, within the bound.
No kernel may reach another device: no remote copies, remote signals or barrier semaphores. Data moves between devices by JAX's collectives and lax.ppermute only.
A program may use at most 64 MiB of HBM per device.

v0:
```python
import math

import jax
import jax.numpy as jnp
from jax import lax
from jax.sharding import PartitionSpec as P


def shifted(value, axis, steps):
    count = lax.axis_size(axis)
    first, last = (max(0, -steps), min(count, count - steps))
    return lax.ppermute(value, axis, [(source, source + steps) for source in range(first, last)])


def dft_tables(tok_rows):
    span_rows = 2 * tok_rows
    frequency = lax.broadcasted_iota(jnp.int32, (span_rows, tok_rows), 0)
    position = lax.broadcasted_iota(jnp.int32, (span_rows, tok_rows), 1)
    angles = (frequency * position % span_rows).astype(jnp.float32) * (2.0 * math.pi / span_rows)
    return (jnp.cos(angles), jnp.sin(angles))


def transform(stacked, cosine, sine):
    block_count, tok_rows, chan_width = stacked.shape
    flat_rows = jnp.transpose(stacked, (1, 0, 2)).reshape(tok_rows, block_count * chan_width)
    real_part = jnp.dot(
        cosine, flat_rows, precision=lax.Precision.HIGHEST, preferred_element_type=jnp.float32
    )
    imag_part = -jnp.dot(
        sine, flat_rows, precision=lax.Precision.HIGHEST, preferred_element_type=jnp.float32
    )
    shape_out = (2 * tok_rows, block_count, chan_width)
    return (real_part.reshape(shape_out), imag_part.reshape(shape_out))


def inverse_single(real_part, imag_part, cosine, sine):
    span_rows = real_part.shape[0]
    result_rows = jnp.dot(
        cosine.T, real_part, precision=lax.Precision.HIGHEST, preferred_element_type=jnp.float32
    )
    result_rows = result_rows - jnp.dot(
        sine.T, imag_part, precision=lax.Precision.HIGHEST, preferred_element_type=jnp.float32
    )
    return result_rows / span_rows


def local(grad_out, out_weight, gate_values, conv_input, conv_output, long_filter, skip_gain):
    tok_rows, chan_width = conv_input.shape
    ctx_count = lax.axis_size("ctx")
    lag_rows = long_filter.shape[0] * ctx_count
    lag_blocks = lag_rows // tok_rows
    dmix = lax.dot_general(
        lax.all_gather(grad_out, "ch", axis=1, tiled=True),
        out_weight,
        (((1,), (1,)), ((), ())),
        preferred_element_type=jnp.float32,
    )
    grad_gate = (dmix * conv_output.astype(jnp.float32)).astype(jnp.bfloat16)
    dsignal = (gate_values.astype(jnp.float32) * dmix).astype(jnp.bfloat16)
    pieces = [dsignal]
    for offset in range(1, lag_blocks + 1):
        pieces.append(shifted(dsignal, "ctx", -offset))
    later = jnp.stack(pieces, 0)
    cosine, sine = dft_tables(tok_rows)
    parity = jnp.where(
        lax.broadcasted_iota(jnp.int32, (2 * tok_rows, 1), 0) % 2 == 0, 1.0, -1.0
    ).astype(jnp.float32)
    later_re, later_im = transform(later.astype(jnp.float32), cosine, sine)
    all_taps = lax.all_gather(long_filter, "ctx", axis=0, tiled=True)
    tap_blocks = all_taps.reshape(lag_blocks, tok_rows, chan_width)
    input_re, input_im = transform(conv_input.astype(jnp.float32)[None], cosine, sine)
    input_re = input_re[:, 0]
    input_im = input_im[:, 0]

    def lag_step(carry, block_index):
        acc_re, acc_im = carry
        near_re = lax.dynamic_index_in_dim(later_re, block_index, 1, keepdims=False)
        near_im = lax.dynamic_index_in_dim(later_im, block_index, 1, keepdims=False)
        next_re = lax.dynamic_index_in_dim(later_re, block_index + 1, 1, keepdims=False)
        next_im = lax.dynamic_index_in_dim(later_im, block_index + 1, 1, keepdims=False)
        pair_re = near_re + parity * next_re
        pair_im = near_im + parity * next_im
        tap_block = lax.dynamic_index_in_dim(tap_blocks, block_index, 0, keepdims=True)
        taps_re, taps_im = transform(tap_block, cosine, sine)
        taps_re = taps_re[:, 0]
        taps_im = taps_im[:, 0]
        acc_re = acc_re + taps_re * pair_re + taps_im * pair_im
        acc_im = acc_im + taps_re * pair_im - taps_im * pair_re
        lag_re = input_re * pair_re + input_im * pair_im
        lag_im = input_re * pair_im - input_im * pair_re
        lag_block = inverse_single(lag_re, lag_im, cosine, sine)
        return ((acc_re, acc_im), lag_block)

    zero_spec = jnp.zeros((2 * tok_rows, chan_width), jnp.float32)
    (corr_re, corr_im), lag_stack = lax.scan(
        lag_step, (zero_spec, zero_spec), jnp.arange(lag_blocks, dtype=jnp.int32)
    )
    corr = inverse_single(corr_re, corr_im, cosine, sine)
    grad_input = (corr + skip_gain * dsignal.astype(jnp.float32)).astype(jnp.bfloat16)
    lag_terms = lag_stack.reshape(lag_rows, chan_width)
    grad_filter = lax.psum_scatter(lag_terms, "ctx", scatter_dimension=0, tiled=True)
    return (grad_input, grad_gate, grad_filter)


def solution(mesh):
    in_specs = (
        P("ctx", "ch"),
        P("ch", None),
        P("ctx", "ch"),
        P("ctx", "ch"),
        P("ctx", "ch"),
        P("ctx", "ch"),
        P("ch"),
    )
    out_specs = (P("ctx", "ch"), P("ctx", "ch"), P("ctx", "ch"))
    return jax.shard_map(local, mesh=mesh, in_specs=in_specs, out_specs=out_specs, check_vma=False)
```

profile of v0, /device:TPU:2, one launch (start us, length us, event | category | flops | bytes accessed | tf_op | source)
XLA Modules:
  0.0 1117.9 jit_solution(11519476099366285835)
XLA Ops:
  10.3 53.5 %all-gather.5.cloned.1.call-done = bf16[128,4096]{1,0:T(8,128)(2,1)} async-done(((bf16[128,256]{1,0:T(8,128)(2,1)}), bf16[128,4096]{1,0:T(8,128)(2,1)}) %all-gather.5.cloned.1.call-update) | async-done | bytes 1048592 | tf_op jit(solution)/shard_map/all_gather | solution.py:53
  63.8 2.7 bitcast_dynamic-update-slice_fusion.16
  66.5 2.5 collective-permute-start
  77.9 5.1 collective-permute-done.1
  85.0 6.0 collective-permute-done.2
  92.9 5.3 collective-permute-done.3
  100.1 6.4 collective-permute-done.4
  108.5 23.4 %collective-permute-done.5 = bf16[128,256]{1,0:T(8,128)(2,1)S(1)} collective-permute-done((bf16[128,256]{1,0:T(8,128)(2,1)}, bf16[128,256]{1,0:T(8,128)(2,1)S(1)}, u32[]{:S(2)}, u32[]{:S(2)}) %collective-permute-start.5) | collective-permute-done | bytes 65568 | tf_op jit(solution)/shard_map/ppermute | solution.py:12
  133.8 9.1 collective-permute-done.6
  144.8 6.7 collective-permute-done.7
  153.4 7.9 collective-permute-done.8
  163.2 17.3 %collective-permute-done.9 = bf16[128,256]{1,0:T(8,128)(2,1)S(1)} collective-permute-done((bf16[128,256]{1,0:T(8,128)(2,1)}, bf16[128,256]{1,0:T(8,128)(2,1)S(1)}, u32[]{:S(2)}, u32[]{:S(2)}) %collective-permute-start.9) | collective-permute-done | bytes 65568 | tf_op jit(solution)/shard_map/ppermute | solution.py:12
  182.4 8.3 collective-permute-done.10
  192.8 6.2 collective-permute-done.11
  202.1 2.3 copy.15
  204.4 5.7 convolution_negate_fusion.1
  210.1 5.7 copy.16
  215.8 5.7 fusion.55
  221.6 187.2 %while.18 = (s32[]{:T(128)}, f32[256,256]{0,1:T(8,128)S(1)}, f32[256,256]{0,1:T(8,128)S(1)}, f32[16,128,256]{2,1,0:T(8,128)}, s32[16]{0:T(128)S(1)}, /*index=5*/...) while((s32[]{:T(128)}, f32[256,256]{0,1:T(8,128)S(1)}, ...), condition=%wide.region_1.2_spmd.clone.clone, body=%wide.region_0.1_spmd.clone.clone.sunk | while | flops 405932032 | bytes 7735593 | solution.py:95
  226.7 1.8 convolution_bitcast_fusion.2
  228.5 2.1 fusion.123
  240.2 2.1 fusion.123
  250.1 1.8 convolution_bitcast_fusion.2
  251.9 2.1 fusion.123
  261.8 1.8 convolution_bitcast_fusion.2
  263.6 2.1 fusion.123
  273.5 1.8 convolution_bitcast_fusion.2
  275.3 2.1 fusion.123
  285.2 1.8 convolution_bitcast_fusion.2
  287.0 2.2 fusion.123
  296.9 1.8 convolution_bitcast_fusion.2
  298.7 2.2 fusion.123
  308.6 1.8 convolution_bitcast_fusion.2
  310.4 2.1 fusion.123
  322.1 2.1 fusion.123
  333.8 2.1 fusion.123
  343.7 1.8 convolution_bitcast_fusion.2
  345.5 2.2 fusion.123
  355.4 1.8 convolution_bitcast_fusion.2
  357.2 2.1 fusion.123
  367.1 1.8 convolution_bitcast_fusion.2
  368.9 2.1 fusion.123
  378.8 1.8 convolution_bitcast_fusion.2
  380.6 2.2 fusion.123
  392.3 2.2 fusion.123
  404.0 2.2 fusion.123
  411.2 2.4 fusion.54
  413.6 697.8 %reduce-scatter.2.cloned.1.call-done = f32[32,256]{1,0:T(8,128)} async-done(((f32[2048,256]{1,0:T(8,128)}), f32[32,256]{1,0:T(8,128)}) %reduce-scatter.2.cloned.1.call-update) | async-done | bytes 32784 | tf_op jit(solution)/shard_map/reduce_scatter | solution.py:101
  (177 shorter events, 96.8 us)
Async XLA Ops:
  7.2 56.7 %copy-start = (bf16[256,4096]{1,0:T(8,128)(2,1)S(1)}, bf16[256,4096]{1,0:T(8,128)(2,1)}, u32[]{:S(2)}) copy-start(bf16[256,4096]{1,0:T(8,128)(2,1)} %param.10) | copy-start | bytes 6291460
  7.2 56.7 %all-gather.5.cloned.1.call-start = ((), (), s32[]{:S(2)}) async-start(), calls=%async_computation.2 | async-start | bytes 1114112 | tf_op jit(solution)/shard_map/all_gather | solution.py:53
  7.9 213.7 %all-gather.3.cloned.1.call-start = ((), (), s32[]{:S(2)}) async-start(), calls=%async_computation.1 | async-start | bytes 2129920 | tf_op jit(solution)/shard_map/all_gather | solution.py:69
  8.7 1102.7 %reduce-scatter.2.cloned.1.call-start = ((), (), s32[]{:S(2)}) async-start(), calls=%async_computation.3 | async-start | bytes 2129920 | tf_op jit(solution)/shard_map/reduce_scatter | solution.py:101
  10.3 58.7 %copy-start.2 = (bf16[128,256]{1,0:T(8,128)(2,1)S(1)}, bf16[128,256]{1,0:T(8,128)(2,1)}, u32[]{:S(2)}) copy-start(bf16[128,256]{1,0:T(8,128)(2,1)} %param.12) | copy-start | bytes 196612
  66.5 8.6 collective-permute-start
  70.0 131.5 %collective-permute-start.15 = (bf16[128,256]{1,0:T(8,128)(2,1)}, bf16[128,256]{1,0:T(8,128)(2,1)S(1)}, u32[]{:S(2)}, u32[]{:S(2)}) collective-permute-start(bf16[128,256]{1,0:T(8,128)(2,1)} %get-tuple-element.297), channel_id=1, source_target_pairs={{256,0},{272,16},{288,32},{304,48},{320,64},{336,80},{352,96},{368... | collective-permute-start | bytes 196616 | tf_op jit(solution)/shard_map/ppermute | solution.py:12
  71.3 129.6 %collective-permute-start.14 = (bf16[128,256]{1,0:T(8,128)(2,1)}, bf16[128,256]{1,0:T(8,128)(2,1)S(1)}, u32[]{:S(2)}, u32[]{:S(2)}) collective-permute-start(bf16[128,256]{1,0:T(8,128)(2,1)} %get-tuple-element.297), channel_id=1, source_target_pairs={{240,0},{256,16},{272,32},{288,48},{304,64},{320,80},{336,96},{352... | collective-permute-start | bytes 196616 | tf_op jit(solution)/shard_map/ppermute | solution.py:12
  72.6 127.7 %collective-permute-start.13 = (bf16[128,256]{1,0:T(8,128)(2,1)}, bf16[128,256]{1,0:T(8,128)(2,1)S(1)}, u32[]{:S(2)}, u32[]{:S(2)}) collective-permute-start(bf16[128,256]{1,0:T(8,128)(2,1)} %get-tuple-element.297), channel_id=1, source_target_pairs={{224,0},{240,16},{256,32},{272,48},{288,64},{304,80},{320,96},{336... | collective-permute-start | bytes 196616 | tf_op jit(solution)/shard_map/ppermute | solution.py:12
  73.9 125.7 %collective-permute-start.12 = (bf16[128,256]{1,0:T(8,128)(2,1)}, bf16[128,256]{1,0:T(8,128)(2,1)S(1)}, u32[]{:S(2)}, u32[]{:S(2)}) collective-permute-start(bf16[128,256]{1,0:T(8,128)(2,1)} %get-tuple-element.297), channel_id=1, source_target_pairs={{208,0},{224,16},{240,32},{256,48},{272,64},{288,80},{304,96},{320... | collective-permute-start | bytes 196616 | tf_op jit(solution)/shard_map/ppermute | solution.py:12
  75.2 7.9 collective-permute-start.1
  83.0 7.9 collective-permute-start.2
  91.0 7.2 collective-permute-start.3
  98.2 8.3 collective-permute-start.4
  106.5 25.3 %collective-permute-start.5 = (bf16[128,256]{1,0:T(8,128)(2,1)}, bf16[128,256]{1,0:T(8,128)(2,1)S(1)}, u32[]{:S(2)}, u32[]{:S(2)}) collective-permute-start(bf16[128,256]{1,0:T(8,128)(2,1)} %get-tuple-element.297), channel_id=1, source_target_pairs={{96,0},{112,16},{128,32},{144,48},{160,64},{176,80},{192,96},{208,... | collective-permute-start | bytes 196616 | tf_op jit(solution)/shard_map/ppermute | solution.py:12
  131.8 11.0 collective-permute-start.6
  142.9 8.6 collective-permute-start.7
  151.5 9.8 collective-permute-start.8
  161.3 19.2 %collective-permute-start.9 = (bf16[128,256]{1,0:T(8,128)(2,1)}, bf16[128,256]{1,0:T(8,128)(2,1)S(1)}, u32[]{:S(2)}, u32[]{:S(2)}) collective-permute-start(bf16[128,256]{1,0:T(8,128)(2,1)} %get-tuple-element.297), channel_id=1, source_target_pairs={{160,0},{176,16},{192,32},{208,48},{224,64},{240,80},{256,96},{272... | collective-permute-start | bytes 196616 | tf_op jit(solution)/shard_map/ppermute | solution.py:12
  180.5 10.2 collective-permute-start.10
  190.7 8.2 collective-permute-start.11
  408.8 0.8 copy-start.1
  408.8 2.4 copy-start.3
Sparse Core Ops, SparseCore 0:
  10.6 53.1 all-gather.4
  67.9 150.4 all-gather.2
  409.0 702.3 reduce-scatter.1
where the time goes:
time: 1120 us
  waiting for transfers between devices  854 us (76%)
  matrix products  110 us (10%)
  loops' own time  73.2 us (7%)
  local copies, waits for them, and re-layouts  41.3 us (4%)
  starting transfers between devices  22 us (2%)
  between operations  14 us (1%)
    reduce_scatter x1, waiting for transfers between devices, local(): lax.psum_scatter(lag_terms, 'ctx', scatter_dimension=0, tiled=True)  698 us
    ppermute x16, waiting for transfers between devices, shifted(): lax.ppermute(value, axis, [(source, source + steps) for source in range(f...  102 us
    another operation x1, loops' own time, local(): lax.scan(lag_step, (zero_spec, zero_spec), jnp.arange(lag_blocks, dtype=j...  73.2 us
    all_gather x1, waiting for transfers between devices, local(): lax.all_gather(grad_out, 'ch', axis=1, tiled=True)  53.5 us
    dot_general x18, matrix products, transform(): jnp.dot(sine, flat_rows, precision=lax.Precision.HIGHEST, preferred_eleme...  41.6 us
    dot_general x18, matrix products, transform(): jnp.dot(cosine, flat_rows, precision=lax.Precision.HIGHEST, preferred_ele...  34.9 us
  transfers between devices with their start and end apart: 19, of which 13 were waited for; matrix products, arithmetic and copies ran while one was open for 4% of the time, Pallas kernels for 0%

commit v1 on v0

v1 whole, which is shorter than its diff:
```python
import functools

import jax
import jax.numpy as jnp
from jax import lax
from jax.experimental import pallas as pl
from jax.experimental.pallas import tpu as pltpu
from jax.sharding import PartitionSpec as P

F32 = jnp.float32
BF16 = jnp.bfloat16
LANES = 128
NT = (((1,), (1,)), ((), ()))

IN_ROWS = 8
OUT_ROWS = 6


def call(body, out_shape, scratch, flops, nbytes):
    return functools.partial(
        pl.pallas_call,
        body,
        out_shape=out_shape,
        scratch_shapes=scratch,
        compiler_params=pltpu.CompilerParams(vmem_limit_bytes=40 * 1024 * 1024),
        cost_estimate=pl.CostEstimate(flops=flops, bytes_accessed=nbytes, transcendentals=0),
    )


def upper(value):
    return value.astype(BF16).astype(F32)


def pack_body(group, conv_ref, taps_ref, out_ref, rows_ref):
    peers, width = rows_ref.shape[0] // IN_ROWS, conv_ref.shape[1]
    turned = conv_ref[...].astype(F32).T
    for j in range(group):
        rows_ref[pl.ds(j, peers, stride=IN_ROWS), :] = turned[j * peers : (j + 1) * peers]
    halves = []
    for start in range(0, width, LANES):
        tile = taps_ref[:, start : start + LANES]
        halves += [tile, pltpu.roll(tile, LANES // 2, 1)]
    taps = jnp.concatenate(halves, axis=0).T[:peers]
    high = upper(taps)
    rows_ref[pl.ds(group, peers, stride=IN_ROWS), :] = high
    rows_ref[pl.ds(group + 1, peers, stride=IN_ROWS), :] = taps - high
    for spare in range(group + 2, IN_ROWS):
        rows_ref[pl.ds(spare, peers, stride=IN_ROWS), :] = jnp.zeros((peers, LANES), F32)
    out_ref[...] = rows_ref[...].astype(BF16)


def gate_body(group, all_ref, weight_ref, gate_ref, conv_ref, grad_gate_ref, out_ref, rows_ref):
    shards, _, depth = all_ref.shape
    peers = rows_ref.shape[0] // group
    dmix = lax.dot_general(all_ref[0], weight_ref[:, :depth], NT, preferred_element_type=F32)
    for s in range(1, shards):
        part = weight_ref[:, s * depth : (s + 1) * depth]
        dmix += lax.dot_general(all_ref[s], part, NT, preferred_element_type=F32)
    grad_gate_ref[...] = (dmix * conv_ref[...].astype(F32)).astype(BF16)
    signal = upper(gate_ref[...].astype(F32) * dmix).T
    for j in range(group):
        rows_ref[pl.ds(j, peers, stride=group), :] = signal[j * peers : (j + 1) * peers]
    out_ref[...] = rows_ref[...].astype(BF16)


def conv_body(
    group, blocks, skip_ref, place_ref, ahead_ref, signal_ref, out_ref,
    ahead_rows, signal_rows, padded, shifted, toeplitz, out_rows,
):
    peers = signal_ref.shape[0] // group
    ahead_rows[...] = ahead_ref[...].astype(F32)
    signal_rows[...] = signal_ref[...].astype(F32)
    row = lax.broadcasted_iota(jnp.int32, (LANES, LANES), 0)
    lane = lax.broadcasted_iota(jnp.int32, (LANES, LANES), 1)
    flip = (row + lane == LANES - 1).astype(BF16)
    below = lane < row
    keep = lane <= row
    tap_lane = lax.broadcasted_iota(jnp.int32, (blocks, LANES), 1) // (LANES // group)
    quarter = LANES // group
    place = place_ref[0]
    tap_rows = []
    for part in range(group):
        high = ahead_rows[pl.ds(part * IN_ROWS + group, blocks, stride=group * IN_ROWS), :]
        low = ahead_rows[pl.ds(part * IN_ROWS + group + 1, blocks, stride=group * IN_ROWS), :]
        tap_rows.append(high + low)
    padded[peers:, :] = jnp.zeros((padded.shape[0] - peers, LANES), F32)
    lag_rows = []
    for j in range(group):
        signal = signal_rows[pl.ds(j, peers, stride=group), :]
        conv = ahead_rows[pl.ds(j, peers, stride=IN_ROWS), :].astype(BF16)
        padded[:peers, :] = signal
        for k in range(blocks + 1):
            shifted[:, k * LANES : (k + 1) * LANES] = padded[k : k + peers, :].astype(BF16)
        taps = jnp.zeros((blocks, LANES), F32)
        for part in range(group):
            moved = pltpu.roll(tap_rows[part], (part - j) % group * quarter, 1)
            taps = jnp.where(tap_lane == part, moved, taps)
        before = jnp.zeros((LANES, LANES), F32)
        for k in range(blocks + 1):
            if k < blocks:
                spread = jnp.broadcast_to(taps[k : k + 1, :], (LANES, LANES))
                now = pltpu.roll(spread, 0, 1, stride=1, stride_axis=0)
            else:
                now = jnp.zeros((LANES, LANES), F32)
            both = jnp.where(below, before, now)
            high = both.astype(BF16)
            toeplitz[:LANES, k * LANES : (k + 1) * LANES] = high
            toeplitz[LANES:, k * LANES : (k + 1) * LANES] = (both - high.astype(F32)).astype(BF16)
            before = now
        corr = lax.dot_general(toeplitz[...], shifted[...], NT, preferred_element_type=F32)
        corr = (corr[:LANES] + corr[LANES:]).T
        gain = skip_ref[j * peers + place]
        out_rows[pl.ds(j, peers, stride=OUT_ROWS), :] = corr + gain * signal
        turned = lax.dot_general(flip, conv, NT, preferred_element_type=F32).astype(BF16)
        products = jnp.dot(turned, shifted[...], preferred_element_type=F32)
        sums = []
        now = pltpu.roll(products[:, :LANES], 1, 1, stride=1, stride_axis=0)
        for k in range(blocks):
            later = pltpu.roll(
                products[:, (k + 1) * LANES : (k + 2) * LANES], 1, 1, stride=1, stride_axis=0
            )
            sums.append(jnp.sum(jnp.where(keep, now, later), axis=0, keepdims=True))
            now = later
        lag_rows.append(jnp.concatenate(sums, axis=0))
    for part in range(group):
        mine = jnp.zeros((blocks, LANES), F32)
        for j in range(group):
            moved = pltpu.roll(lag_rows[j], (j - part) % group * quarter, 1)
            mine = jnp.where(tap_lane == j, moved, mine)
        high = upper(mine)
        out_rows[pl.ds(part * OUT_ROWS + group, blocks, stride=group * OUT_ROWS), :] = high
        out_rows[pl.ds(part * OUT_ROWS + group + 1, blocks, stride=group * OUT_ROWS), :] = mine - high
    out_ref[...] = out_rows[...].astype(BF16)


def unpack_body(group, back_ref, grad_input_ref, grad_filter_ref, rows_ref):
    peers = rows_ref.shape[0] // OUT_ROWS
    rows_ref[...] = back_ref[...].astype(F32)
    parts = [rows_ref[pl.ds(j, peers, stride=OUT_ROWS), :] for j in range(group)]
    grad_input_ref[...] = jnp.concatenate(parts, axis=0).T.astype(BF16)
    lags = rows_ref[pl.ds(group, peers, stride=OUT_ROWS), :] + rows_ref[pl.ds(group + 1, peers, stride=OUT_ROWS), :]
    turned = jnp.concatenate([lags, lags], axis=0).T
    quarter = LANES // group
    left = lax.broadcasted_iota(jnp.int32, (quarter, LANES), 1) < peers
    for pair in range(group // 2):
        even = turned[2 * pair * quarter : (2 * pair + 1) * quarter]
        odd = turned[(2 * pair + 1) * quarter : (2 * pair + 2) * quarter]
        grad_filter_ref[:, pair * LANES : (pair + 1) * LANES] = jnp.where(left, even, odd)


def local(grad_out, out_weight, gate_values, conv_input, conv_output, long_filter, skip_gain):
    tok_rows, chan_width = conv_input.shape
    peers = lax.axis_size("ctx")
    group = chan_width // peers
    lag_rows = long_filter.shape[0]
    blocks = lag_rows * peers // tok_rows
    place = lax.axis_index("ctx").astype(jnp.int32).reshape(1)
    vmem = pltpu.VMEM
    shape = jax.ShapeDtypeStruct

    gathered = lax.all_gather(grad_out, "ch", axis=0, tiled=False)

    ahead = call(
        functools.partial(pack_body, group),
        shape((peers * IN_ROWS, tok_rows), BF16),
        [vmem((peers * IN_ROWS, tok_rows), F32)],
        0,
        200_000,
    )()(conv_input, long_filter)
    ahead = lax.all_to_all(ahead.reshape(peers, IN_ROWS, tok_rows), "ctx", 0, 0, tiled=True)

    grad_gate, signal = call(
        functools.partial(gate_body, group),
        (shape((tok_rows, chan_width), BF16), shape((chan_width, tok_rows), BF16)),
        [vmem((chan_width, tok_rows), F32)],
        2 * tok_rows * out_weight.size,
        2 * out_weight.size,
    )()(gathered, out_weight, gate_values, conv_output)
    signal = lax.all_to_all(signal.reshape(peers, group, tok_rows), "ctx", 0, 0, tiled=True)

    span = (blocks + 1) * tok_rows
    smem = pl.BlockSpec(memory_space=pltpu.SMEM)
    whole = pl.BlockSpec(memory_space=pltpu.VMEM)
    back = call(
        functools.partial(conv_body, group, blocks),
        shape((peers * OUT_ROWS, tok_rows), BF16),
        [
            vmem((peers * IN_ROWS, tok_rows), F32),
            vmem((peers * group, tok_rows), F32),
            vmem((peers + blocks, tok_rows), F32),
            vmem((peers, span), BF16),
            vmem((2 * tok_rows, span), BF16),
            vmem((peers * OUT_ROWS, tok_rows), F32),
        ],
        6 * group * peers * tok_rows * span,
        1_000_000,
    )(in_specs=[smem, smem, whole, whole])(
        skip_gain,
        place,
        ahead.reshape(peers * IN_ROWS, tok_rows),
        signal.reshape(peers * group, tok_rows),
    )
    back = lax.all_to_all(back.reshape(peers, OUT_ROWS, tok_rows), "ctx", 0, 0, tiled=True)
    grad_input, grad_filter = call(
        functools.partial(unpack_body, group),
        (shape((tok_rows, chan_width), BF16), shape((lag_rows, chan_width), F32)),
        [vmem((peers * OUT_ROWS, tok_rows), F32)],
        0,
        300_000,
    )()(back.reshape(peers * OUT_ROWS, tok_rows))
    return grad_input, grad_gate, grad_filter


def solution(mesh):
    in_specs = (
        P("ctx", "ch"),
        P("ch", None),
        P("ctx", "ch"),
        P("ctx", "ch"),
        P("ctx", "ch"),
        P("ctx", "ch"),
        P("ch"),
    )
    out_specs = (P("ctx", "ch"), P("ctx", "ch"), P("ctx", "ch"))
    return jax.shard_map(local, mesh=mesh, in_specs=in_specs, out_specs=out_specs, check_vma=False)
```

time: 1120 us -> 136 us (0.12)
  the two profiles are of different devices: /device:TPU:2 before, /device:TPU:24 now
where the time goes in v1:
time: 136 us; the launch traced here: 135 us
  waiting for transfers between devices  47.8 us (35%)
  starting transfers between devices  38.6 us (28%)
  blocking collectives  21.1 us (16%)
  between operations  14.1 us (10%)
  Pallas kernels  7.29 us (5%)
  local copies, waits for them, and re-layouts  6.16 us (5%)
    all_gather x1, waiting for transfers between devices, local(): gathered = lax.all_gather(grad_out, 'ch', axis=0, tiled=False)  31.7 us
    all_to_all x1, starting transfers between devices, local(): lax.all_to_all(ahead.reshape(peers, IN_ROWS, tok_rows), 'ctx', 0, 0, tile...  22.2 us
    all_to_all x1, blocking collectives, local(): lax.all_to_all(back.reshape(peers, OUT_ROWS, tok_rows), 'ctx', 0, 0, tile...  21.1 us
    all_to_all x1, starting transfers between devices, local(): lax.all_to_all(signal.reshape(peers, group, tok_rows), 'ctx', 0, 0, tiled...  16.3 us
    all_to_all x1, waiting for transfers between devices, local(): lax.all_to_all(signal.reshape(peers, group, tok_rows), 'ctx', 0, 0, tiled...  15.4 us
    unnamed x14, local copies, waits for them, and re-layouts  6.09 us
    pallas_call x1, Pallas kernels, local(): call(functools.partial(conv_body, group, blocks), shape((peers * OUT_ROWS...  4.19 us
  transfers between devices with their start and end apart: 3, of which 2 were waited for; matrix products, arithmetic and copies ran while one was open for 0% of the time, Pallas kernels for 2%

profile of v1, /device:TPU:24, one launch (start us, length us, event | category | flops | bytes accessed | tf_op | source)
XLA Modules:
  0.0 135.0 jit_solution(6696318458609660375)
XLA Ops:
  7.2 0.0 copy-start.6
  7.2 0.0 all-gather.3.cloned.1.call-start
  7.2 0.7 all-gather.3.cloned.1.call-update
  7.9 0.0 copy-start.2
  7.9 0.8 copy-done.2
  8.8 0.0 copy-start.5
  8.8 0.8 copy-done.5
  9.5 0.8 shard_map.94
  10.3 22.2 %all-to-all-start = ((bf16[64,8,128]{2,1,0:T(8,128)(2,1)}), bf16[64,8,128]{2,1,0:T(8,128)(2,1)S(1)}, u32[]{:S(2)}, u32[]{:S(2)}) async-start(bf16[64,8,128]{2,1,0:T(8,128)(2,1)} %bitcast.1), calls=%async_computation | async-start | bytes 262144 | tf_op jit(solution)/shard_map/all_to_all | solution.py:170
  32.6 31.7 %all-gather.3.cloned.1.call-done = bf16[2048,256]{1,0:T(8,128)(2,1)} async-done(((bf16[128,256]{1,0:T(8,128)(2,1)}), bf16[2048,256]{1,0:T(8,128)(2,1)}) %all-gather.3.cloned.1.call-update) | async-done | bytes 1048592 | tf_op jit(solution)/shard_map/all_gather | solution.py:161
  64.3 0.0 copy-start
  64.3 1.6 %copy-done = bf16[256,4096]{1,0:T(8,128)(2,1)S(1)} copy-done((bf16[256,4096]{1,0:T(8,128)(2,1)S(1)}, bf16[256,4096]{1,0:T(8,128)(2,1)}, u32[]{:S(2)}) %copy-start) | copy-done | bytes 2097176
  65.8 0.0 copy-start.1
  65.8 1.2 copy-done.1
  67.1 0.0 copy-start.3
  67.1 0.8 copy-done.3
  67.9 0.0 copy-start.4
  67.9 0.8 copy-done.4
  68.8 1.5 %shard_map.95 = (bf16[128,256]{1,0:T(8,128)(2,1)}, bf16[256,128]{1,0:T(8,128)(2,1)}) custom-call(bf16[16,128,256]{2,1,0:T(8,128)(2,1)S(1)} %bitcast.6, bf16[256,4096]{1,0:T(8,128)(2,1)S(1)} %copy-done, bf16[128,256]{1,0:T(8,128)(2,1)S(1)} %copy-done.3, bf16[128,256]{1,0:T(8,128)(2,1)S(1)} %copy-done.4), custom_call_target="tpu_custom_call" | custom-call | flops 268435456 | bytes 2097152 | tf_op jit(solution)/shard_map/pallas_call | solution.py:172
  70.3 0.0 all-to-all-done
  70.3 16.3 %all-to-all-start.1 = ((bf16[64,4,128]{2,1,0:T(4,128)(2,1)}), bf16[64,4,128]{2,1,0:T(4,128)(2,1)S(1)}, u32[]{:S(2)}, u32[]{:S(2)}) async-start(bf16[64,4,128]{2,1,0:T(4,128)(2,1)} %bitcast.4), calls=%async_computation.1 | async-start | bytes 131072 | tf_op jit(solution)/shard_map/all_to_all | solution.py:179
  86.6 15.4 %all-to-all-done.1 = bf16[64,4,128]{2,1,0:T(4,128)(2,1)S(1)} async-done(((bf16[64,4,128]{2,1,0:T(4,128)(2,1)}), bf16[64,4,128]{2,1,0:T(4,128)(2,1)S(1)}, u32[]{:S(2)}, u32[]{:S(2)}) %all-to-all-start.1) | async-done | bytes 65568 | tf_op jit(solution)/shard_map/all_to_all | solution.py:179
  102.1 0.0 copy-done.6
  102.1 4.2 %shard_map.96 = bf16[384,128]{1,0:T(8,128)(2,1)S(1)} custom-call(f32[256]{0:T(256)S(1)} %copy-done.6, s32[1]{0:T(128)} %bitcast.place_ref, bf16[512,128]{1,0:T(8,128)(2,1)S(1)} %bitcast.7, bf16[256,128]{1,0:T(8,128)(2,1)S(1)} %bitcast.8), custom_call_target="tpu_custom_call" | custom-call | flops 427819008 | bytes 1000000 | tf_op jit(solution)/shard_map/pallas_call | solution.py:184
  106.3 21.1 %all_to_all.15 = bf16[64,6,128]{2,1,0:T(8,128)(2,1)S(1)} all-to-all(bf16[64,6,128]{2,1,0:T(8,128)(2,1)S(1)} %reshape.32), channel_id=1, replica_groups=mesh['ctx'=64,'ch'=16] {'ctx'}, dimensions={0} | all-to-all | bytes 196608 | tf_op jit(solution)/shard_map/all_to_all | solution.py:203
  127.4 0.8 shard_map.97
  (2 shorter events, 0.1 us)
Async XLA Ops:
  7.2 94.9 %copy-start.6 = (f32[256]{0:T(256)S(1)}, f32[256]{0:T(256)}, u32[]{:S(2)}) copy-start(f32[256]{0:T(256)} %skip_ref.1) | copy-start | bytes 3076
  7.2 57.1 %all-gather.3.cloned.1.call-start = ((), (), s32[]{:S(2)}) async-start(), calls=%async_computation.3 | async-start | bytes 1114112 | tf_op jit(solution)/shard_map/all_gather | solution.py:161
  7.9 0.8 copy-start.2
  8.8 0.8 copy-start.5
  10.3 60.0 %all-to-all-start = ((bf16[64,8,128]{2,1,0:T(8,128)(2,1)}), bf16[64,8,128]{2,1,0:T(8,128)(2,1)S(1)}, u32[]{:S(2)}, u32[]{:S(2)}) async-start(bf16[64,8,128]{2,1,0:T(8,128)(2,1)} %bitcast.1), calls=%async_computation | async-start | bytes 262144 | tf_op jit(solution)/shard_map/all_to_all | solution.py:170
  64.3 1.6 %copy-start = (bf16[256,4096]{1,0:T(8,128)(2,1)S(1)}, bf16[256,4096]{1,0:T(8,128)(2,1)}, u32[]{:S(2)}) copy-start(bf16[256,4096]{1,0:T(8,128)(2,1)} %weight_ref.1) | copy-start | bytes 6291460
  65.8 1.2 copy-start.1
  67.1 0.8 copy-start.3
  67.9 0.8 copy-start.4
  70.3 31.8 %all-to-all-start.1 = ((bf16[64,4,128]{2,1,0:T(4,128)(2,1)}), bf16[64,4,128]{2,1,0:T(4,128)(2,1)S(1)}, u32[]{:S(2)}, u32[]{:S(2)}) async-start(bf16[64,4,128]{2,1,0:T(4,128)(2,1)} %bitcast.4), calls=%async_computation.1 | async-start | bytes 131072 | tf_op jit(solution)/shard_map/all_to_all | solution.py:179
Sparse Core Ops, SparseCore 0:
  10.7 53.4 all-gather.2

commit v2 on v1

--- a/solution.py
+++ b/solution.py
@@ -12,7 +12,7 @@
 LANES = 128
 NT = (((1,), (1,)), ((), ()))
 
-IN_ROWS = 8
+IN_ROWS = 10
 OUT_ROWS = 6
 
 
@@ -31,45 +31,79 @@
     return value.astype(BF16).astype(F32)
 
 
-def pack_body(group, conv_ref, taps_ref, out_ref, rows_ref):
-    peers, width = rows_ref.shape[0] // IN_ROWS, conv_ref.shape[1]
-    turned = conv_ref[...].astype(F32).T
-    for j in range(group):
-        rows_ref[pl.ds(j, peers, stride=IN_ROWS), :] = turned[j * peers : (j + 1) * peers]
+def first_body(
+    group, core_ref, mine_ref, weight_hbm, gate_hbm, conv_out_hbm, conv_hbm, taps_hbm,
+    part_ref, weight_ref, gate_ref, conv_out_ref, conv_turned_ref, taps_ref,
+    weight_mine, conv_here, taps_here, mine_sems, other_sems, sems,
+):
+    chips, _, depth = mine_ref.shape
+    peers = taps_ref.shape[1]
+    width = conv_here.shape[1]
+    core = core_ref[0]
+
+    def columns(parity, chip, target, sem):
+        first = pl.multiple_of((2 * chip + parity) * depth, depth)
+        inside = target.at[:, chip * depth : (chip + 1) * depth]
+        return pltpu.make_async_copy(weight_hbm.at[:, pl.ds(first, depth)], inside, sem.at[chip])
+
+    mine = [columns(core, chip, weight_mine, mine_sems) for chip in range(chips)]
+    small = [
+        pltpu.make_async_copy(conv_hbm, conv_here, sems.at[0]),
+        pltpu.make_async_copy(taps_hbm, taps_here, sems.at[1]),
+        pltpu.make_async_copy(gate_hbm, gate_ref, sems.at[2]),
+        pltpu.make_async_copy(conv_out_hbm, conv_out_ref, sems.at[3]),
+    ]
+    other = [columns(1 - core, chip, weight_ref, other_sems) for chip in range(chips)]
+    for copy in small[:2] + mine + small[2:] + other:
+        copy.start()
+    small[0].wait()
+    conv_turned_ref[...] = conv_here[...].astype(F32).T
+    small[1].wait()
     halves = []
     for start in range(0, width, LANES):
-        tile = taps_ref[:, start : start + LANES]
+        tile = taps_here[:, start : start + LANES]
         halves += [tile, pltpu.roll(tile, LANES // 2, 1)]
     taps = jnp.concatenate(halves, axis=0).T[:peers]
     high = upper(taps)
-    rows_ref[pl.ds(group, peers, stride=IN_ROWS), :] = high
-    rows_ref[pl.ds(group + 1, peers, stride=IN_ROWS), :] = taps - high
-    for spare in range(group + 2, IN_ROWS):
-        rows_ref[pl.ds(spare, peers, stride=IN_ROWS), :] = jnp.zeros((peers, LANES), F32)
-    out_ref[...] = rows_ref[...].astype(BF16)
-
-
-def gate_body(group, all_ref, weight_ref, gate_ref, conv_ref, grad_gate_ref, out_ref, rows_ref):
-    shards, _, depth = all_ref.shape
-    peers = rows_ref.shape[0] // group
-    dmix = lax.dot_general(all_ref[0], weight_ref[:, :depth], NT, preferred_element_type=F32)
-    for s in range(1, shards):
-        part = weight_ref[:, s * depth : (s + 1) * depth]
-        dmix += lax.dot_general(all_ref[s], part, NT, preferred_element_type=F32)
-    grad_gate_ref[...] = (dmix * conv_ref[...].astype(F32)).astype(BF16)
+    taps_ref[0] = high
+    taps_ref[1] = taps - high
+    total = None
+    for chip in range(chips):
+        mine[chip].wait()
+        part = weight_mine[:, chip * depth : (chip + 1) * depth]
+        term = lax.dot_general(mine_ref[chip], part, NT, preferred_element_type=F32)
+        total = term if total is None else total + term
+    part_ref[...] = total
+    for copy in small[2:] + other:
+        copy.wait()
+
+
+def second_body(
+    group, other_ref, part_ref, weight_ref, gate_ref, conv_out_ref, conv_turned_ref, taps_ref,
+    grad_gate_ref, out_ref, rows_ref,
+):
+    chips, _, depth = other_ref.shape
+    peers = rows_ref.shape[0] // IN_ROWS
+    dmix = part_ref[...]
+    for chip in range(chips):
+        part = weight_ref[:, chip * depth : (chip + 1) * depth]
+        dmix += lax.dot_general(other_ref[chip], part, NT, preferred_element_type=F32)
+    grad_gate_ref[...] = (dmix * conv_out_ref[...].astype(F32)).astype(BF16)
     signal = upper(gate_ref[...].astype(F32) * dmix).T
     for j in range(group):
-        rows_ref[pl.ds(j, peers, stride=group), :] = signal[j * peers : (j + 1) * peers]
+        rows_ref[pl.ds(j, peers, stride=IN_ROWS), :] = conv_turned_ref[j * peers : (j + 1) * peers]
+        rows_ref[pl.ds(group + 2 + j, peers, stride=IN_ROWS), :] = signal[j * peers : (j + 1) * peers]
+    rows_ref[pl.ds(group, peers, stride=IN_ROWS), :] = taps_ref[0]
+    rows_ref[pl.ds(group + 1, peers, stride=IN_ROWS), :] = taps_ref[1]
     out_ref[...] = rows_ref[...].astype(BF16)
 
 
 def conv_body(
-    group, blocks, skip_ref, place_ref, ahead_ref, signal_ref, out_ref,
-    ahead_rows, signal_rows, padded, shifted, toeplitz, out_rows,
+    group, blocks, skip_ref, place_ref, in_ref, out_ref,
+    in_rows, padded, shifted, toeplitz, out_rows,
 ):
-    peers = signal_ref.shape[0] // group
-    ahead_rows[...] = ahead_ref[...].astype(F32)
-    signal_rows[...] = signal_ref[...].astype(F32)
+    peers = in_rows.shape[0] // IN_ROWS
+    in_rows[...] = in_ref[...].astype(F32)
     row = lax.broadcasted_iota(jnp.int32, (LANES, LANES), 0)
     lane = lax.broadcasted_iota(jnp.int32, (LANES, LANES), 1)
     flip = (row + lane == LANES - 1).astype(BF16)
@@ -80,14 +114,14 @@
     place = place_ref[0]
     tap_rows = []
     for part in range(group):
-        high = ahead_rows[pl.ds(part * IN_ROWS + group, blocks, stride=group * IN_ROWS), :]
-        low = ahead_rows[pl.ds(part * IN_ROWS + group + 1, blocks, stride=group * IN_ROWS), :]
+        high = in_rows[pl.ds(part * IN_ROWS + group, blocks, stride=group * IN_ROWS), :]
+        low = in_rows[pl.ds(part * IN_ROWS + group + 1, blocks, stride=group * IN_ROWS), :]
         tap_rows.append(high + low)
     padded[peers:, :] = jnp.zeros((padded.shape[0] - peers, LANES), F32)
     lag_rows = []
     for j in range(group):
-        signal = signal_rows[pl.ds(j, peers, stride=group), :]
-        conv = ahead_rows[pl.ds(j, peers, stride=IN_ROWS), :].astype(BF16)
+        signal = in_rows[pl.ds(group + 2 + j, peers, stride=IN_ROWS), :]
+        conv = in_rows[pl.ds(j, peers, stride=IN_ROWS), :].astype(BF16)
         padded[:peers, :] = signal
         for k in range(blocks + 1):
             shifted[:, k * LANES : (k + 1) * LANES] = padded[k : k + peers, :].astype(BF16)
@@ -148,6 +182,12 @@
         grad_filter_ref[:, pair * LANES : (pair + 1) * LANES] = jnp.where(left, even, odd)
 
 
+def exchange(rows, count):
+    peers = lax.axis_size("ctx")
+    pairs = rows.reshape(peers, count // 2, 2, rows.shape[1])
+    return lax.all_to_all(pairs, "ctx", 0, 0, tiled=True).reshape(rows.shape)
+
+
 def local(grad_out, out_weight, gate_values, conv_input, conv_output, long_filter, skip_gain):
     tok_rows, chan_width = conv_input.shape
     peers = lax.axis_size("ctx")
@@ -157,36 +197,59 @@
     place = lax.axis_index("ctx").astype(jnp.int32).reshape(1)
     vmem = pltpu.VMEM
     shape = jax.ShapeDtypeStruct
-
-    gathered = lax.all_gather(grad_out, "ch", axis=0, tiled=False)
-
-    ahead = call(
-        functools.partial(pack_body, group),
-        shape((peers * IN_ROWS, tok_rows), BF16),
-        [vmem((peers * IN_ROWS, tok_rows), F32)],
-        0,
-        200_000,
-    )()(conv_input, long_filter)
-    ahead = lax.all_to_all(ahead.reshape(peers, IN_ROWS, tok_rows), "ctx", 0, 0, tiled=True)
-
-    grad_gate, signal = call(
-        functools.partial(gate_body, group),
-        (shape((tok_rows, chan_width), BF16), shape((chan_width, tok_rows), BF16)),
-        [vmem((chan_width, tok_rows), F32)],
-        2 * tok_rows * out_weight.size,
-        2 * out_weight.size,
-    )()(gathered, out_weight, gate_values, conv_output)
-    signal = lax.all_to_all(signal.reshape(peers, group, tok_rows), "ctx", 0, 0, tiled=True)
-
-    span = (blocks + 1) * tok_rows
     smem = pl.BlockSpec(memory_space=pltpu.SMEM)
     whole = pl.BlockSpec(memory_space=pltpu.VMEM)
+
+    chips = lax.axis_size("ch") // 2
+    core = (lax.axis_index("ch") % 2).astype(jnp.int32).reshape(1)
+    sides = [[2 * chip + side for chip in range(chips)] for side in range(2)]
+    copies = jnp.broadcast_to(grad_out[None], (chips, tok_rows, chan_width))
+    mine = lax.all_to_all(copies, "ch", 0, 0, tiled=True, axis_index_groups=sides)
+    other = lax.ppermute(mine, "ch", [(i, i ^ 1) for i in range(2 * chips)])
+
+    hbm = pl.BlockSpec(memory_space=pltpu.HBM)
+    dma = pltpu.SemaphoreType.DMA
+    half = chips * chan_width
+    local_shape = (tok_rows, chan_width)
+    stored = (out_weight, gate_values, conv_output, conv_input, long_filter)
+    ready = call(
+        functools.partial(first_body, group),
+        (
+            shape(local_shape, F32),
+            shape((chan_width, half), BF16),
+            shape(local_shape, BF16),
+            shape(local_shape, BF16),
+            shape((chan_width, tok_rows), F32),
+            shape((2, peers, tok_rows), F32),
+        ),
+        [
+            vmem((chan_width, half), BF16),
+            vmem(local_shape, BF16),
+            vmem((lag_rows, chan_width), F32),
+            dma((chips,)),
+            dma((chips,)),
+            dma((4,)),
+        ],
+        tok_rows * out_weight.size,
+        2 * out_weight.size,
+    )(in_specs=[smem, whole] + [hbm] * 5)(
+        core, mine, *(pltpu.with_memory_space_constraint(held, pltpu.HBM) for held in stored)
+    )
+    grad_gate, rows = call(
+        functools.partial(second_body, group),
+        (shape(local_shape, BF16), shape((peers * IN_ROWS, tok_rows), BF16)),
+        [vmem((peers * IN_ROWS, tok_rows), F32)],
+        tok_rows * out_weight.size,
+        2 * out_weight.size,
+    )()(other, *ready)
+    rows = exchange(rows, IN_ROWS)
+
+    span = (blocks + 1) * tok_rows
     back = call(
         functools.partial(conv_body, group, blocks),
         shape((peers * OUT_ROWS, tok_rows), BF16),
         [
             vmem((peers * IN_ROWS, tok_rows), F32),
-            vmem((peers * group, tok_rows), F32),
             vmem((peers + blocks, tok_rows), F32),
             vmem((peers, span), BF16),
             vmem((2 * tok_rows, span), BF16),
@@ -194,20 +257,15 @@
         ],
         6 * group * peers * tok_rows * span,
         1_000_000,
-    )(in_specs=[smem, smem, whole, whole])(
-        skip_gain,
-        place,
-        ahead.reshape(peers * IN_ROWS, tok_rows),
-        signal.reshape(peers * group, tok_rows),
-    )
-    back = lax.all_to_all(back.reshape(peers, OUT_ROWS, tok_rows), "ctx", 0, 0, tiled=True)
+    )(in_specs=[smem, smem, whole])(skip_gain, place, rows)
+    back = exchange(back, OUT_ROWS)
     grad_input, grad_filter = call(
         functools.partial(unpack_body, group),
         (shape((tok_rows, chan_width), BF16), shape((lag_rows, chan_width), F32)),
         [vmem((peers * OUT_ROWS, tok_rows), F32)],
         0,
         300_000,
-    )()(back.reshape(peers * OUT_ROWS, tok_rows))
+    )()(back)
     return grad_input, grad_gate, grad_filter
 
 

time: 136 us -> 98.1 us (0.72)
  the two profiles are of different devices: /device:TPU:24 before, /device:TPU:2 now
where the time goes in v2:
time: 98.1 us; the launch traced here: 97.8 us
  blocking collectives  44.5 us (45%)
  starting transfers between devices  24.2 us (25%)
  waiting for transfers between devices  18.5 us (19%)
  Pallas kernels  8.95 us (9%)
    all_to_all x1, blocking collectives, local(): lax.all_to_all(copies, 'ch', 0, 0, tiled=True, axis_index_groups=sides)  24.4 us
    all_to_all x1, starting transfers between devices, exchange(): return lax.all_to_all(pairs, 'ctx', 0, 0, tiled=True).reshape(rows.shape)  22.3 us
    all_to_all x1, blocking collectives, exchange(): return lax.all_to_all(pairs, 'ctx', 0, 0, tiled=True).reshape(rows.shape)  20.1 us
    all_to_all x1, waiting for transfers between devices, exchange(): return lax.all_to_all(pairs, 'ctx', 0, 0, tiled=True).reshape(rows.shape)  18.5 us
    pallas_call x1, Pallas kernels, local(): call(functools.partial(conv_body, group, blocks), shape((peers * OUT_ROWS...  4.2 us
    pallas_call x1, Pallas kernels, local(): call(functools.partial(first_body, group), (shape(local_shape, F32), shap...  2.75 us
  transfers between devices with their start and end apart: 2, of which 1 were waited for; matrix products, arithmetic and copies ran while one was open for 0% of the time, Pallas kernels for 3%

profile of v2, /device:TPU:2, one launch (start us, length us, event | category | flops | bytes accessed | tf_op | source)
XLA Modules:
  0.0 97.8 jit_solution(15421359593910759531)
XLA Ops:
  0.6 0.9 broadcast_in_dim.2
  1.5 24.4 %all_to_all.15.mine_ref = bf16[8,128,256]{2,1,0:T(8,128)(2,1)S(1)} all-to-all(bf16[8,128,256]{2,1,0:T(8,128)(2,1)S(1)} %broadcast_in_dim.2), channel_id=1, replica_groups={{0,2,4,6,8,10,12,14},{1,3,5,7,9,11,13,15},{16,18,20,22,24,26,28,30},{17..., dimensions={0} | all-to-all | bytes 1048576 | tf_op jit(solution)/shard_map/all_to_all | solution.py:207
  25.9 1.9 %collective-permute-start = (bf16[8,128,256]{2,1,0:T(8,128)(2,1)S(1)}, bf16[8,128,256]{2,1,0:T(8,128)(2,1)S(1)}, u32[]{:S(2)}, u32[]{:S(2)}) collective-permute-start(bf16[8,128,256]{2,1,0:T(8,128)(2,1)S(1)} %all_to_all.15.mine_ref), channel_id=1, source_target_pairs={{0,1},{1,0},{2,3},{3,2},{4,5},{5,4},{6,7},{7,6},{8,9},{9,8},{10,11... | collective-permute-start | bytes 1572872 | tf_op jit(solution)/shard_map/ppermute | solution.py:208
  27.8 0.0 copy-start
  27.8 2.7 %shard_map.94 = (f32[128,256]{1,0:T(8,128)S(1)}, bf16[256,2048]{1,0:T(8,128)(2,1)S(1)}, bf16[128,256]{1,0:T(8,128)(2,1)S(1)}, bf16[128,256]{1,0:T(8,128)(2,1)S(1...) custom-call(s32[1]{0:T(128)} %bitcast.1.core_ref, bf16[8,128,256]{2,1,0:T(8,128)(2,1)S(1)} %all_to_all.15.mine_ref, ...), custom_call_target="tpu_custom_call" | custom-call | flops 134217728 | bytes 2097152 | tf_op jit(solution)/shard_map/pallas_call | solution.py:215
  30.6 0.0 collective-permute-done.other_ref
  30.6 1.2 %shard_map.95 = (bf16[128,256]{1,0:T(8,128)(2,1)}, bf16[640,128]{1,0:T(8,128)(2,1)}) custom-call(bf16[8,128,256]{2,1,0:T(8,128)(2,1)S(1)} %collective-permute-done.other_ref, f32[128,256]{1,0:T(8,128)S(1)} %get-tuple-element.13.part_ref, bf16[256,2048]{1,0:T(8,128)(2,1)S(1)} %get-tuple-element.14.weight_ref, ...), custom_call_target="tpu_custom_call" | custom-call | flops 134217728 | bytes 2097152 | tf_op jit(solution)/shard_map/pallas_call | solution.py:238
  31.9 22.3 %all-to-all-start.1 = ((bf16[64,5,2,128]{3,2,1,0:T(2,128)(2,1)}), bf16[64,5,2,128]{3,2,1,0:T(2,128)(2,1)S(1)}, u32[]{:S(2)}, u32[]{:S(2)}) async-start(bf16[64,5,2,128]{3,2,1,0:T(2,128)(2,1)} %bitcast.2), calls=%async_computation.1 | async-start | bytes 327680 | tf_op jit(solution)/shard_map/all_to_all | solution.py:188
  54.2 18.5 %all-to-all-done.1 = bf16[64,5,2,128]{3,2,1,0:T(2,128)(2,1)S(1)} async-done(((bf16[64,5,2,128]{3,2,1,0:T(2,128)(2,1)}), bf16[64,5,2,128]{3,2,1,0:T(2,128)(2,1)S(1)}, u32[]{:S(2)}, u32[]{:S(2)}) %all-to-all-start.1) | async-done | bytes 163872 | tf_op jit(solution)/shard_map/all_to_all | solution.py:188
  72.7 0.0 copy-done
  72.7 4.2 %shard_map.96 = bf16[384,128]{1,0:T(8,128)(2,1)S(1)} custom-call(f32[256]{0:T(256)S(1)} %copy-done, s32[1]{0:T(128)} %bitcast.place_ref, bf16[640,128]{1,0:T(8,128)(2,1)S(1)} %bitcast.7), custom_call_target="tpu_custom_call" | custom-call | flops 427819008 | bytes 1000000 | tf_op jit(solution)/shard_map/pallas_call | solution.py:248
  76.9 20.1 %all_to_all.16 = bf16[64,3,2,128]{3,2,1,0:T(2,128)(2,1)S(1)} all-to-all(bf16[64,3,2,128]{3,2,1,0:T(2,128)(2,1)S(1)} %bitcast.8), channel_id=1, replica_groups=mesh['ctx'=64,'ch'=16] {'ctx'}, dimensions={0} | all-to-all | bytes 196608 | tf_op jit(solution)/shard_map/all_to_all | solution.py:188
  97.0 0.8 shard_map.97
Async XLA Ops:
  25.9 4.7 %collective-permute-start = (bf16[8,128,256]{2,1,0:T(8,128)(2,1)S(1)}, bf16[8,128,256]{2,1,0:T(8,128)(2,1)S(1)}, u32[]{:S(2)}, u32[]{:S(2)}) collective-permute-start(bf16[8,128,256]{2,1,0:T(8,128)(2,1)S(1)} %all_to_all.15.mine_ref), channel_id=1, source_target_pairs={{0,1},{1,0},{2,3},{3,2},{4,5},{5,4},{6,7},{7,6},{8,9},{9,8},{10,11... | collective-permute-start | bytes 1572872 | tf_op jit(solution)/shard_map/ppermute | solution.py:208
  27.8 44.9 %copy-start = (f32[256]{0:T(256)S(1)}, f32[256]{0:T(256)}, u32[]{:S(2)}) copy-start(f32[256]{0:T(256)} %skip_ref.1) | copy-start | bytes 3076
  31.9 40.9 %all-to-all-start.1 = ((bf16[64,5,2,128]{3,2,1,0:T(2,128)(2,1)}), bf16[64,5,2,128]{3,2,1,0:T(2,128)(2,1)S(1)}, u32[]{:S(2)}, u32[]{:S(2)}) async-start(bf16[64,5,2,128]{3,2,1,0:T(2,128)(2,1)} %bitcast.2), calls=%async_computation.1 | async-start | bytes 327680 | tf_op jit(solution)/shard_map/all_to_all | solution.py:188

commit v3 on v2

--- a/solution.py
+++ b/solution.py
@@ -10,6 +10,7 @@
 F32 = jnp.float32
 BF16 = jnp.bfloat16
 LANES = 128
+PART = 64
 NT = (((1,), (1,)), ((), ()))
 
 IN_ROWS = 10
@@ -68,10 +69,14 @@
     taps_ref[0] = high
     taps_ref[1] = taps - high
     total = None
-    for chip in range(chips):
-        mine[chip].wait()
-        part = weight_mine[:, chip * depth : (chip + 1) * depth]
-        term = lax.dot_general(mine_ref[chip], part, NT, preferred_element_type=F32)
+    step = chips // 2
+    for start in range(0, chips, step):
+        some = range(start, start + step)
+        for chip in some:
+            mine[chip].wait()
+        rows = jnp.concatenate([mine_ref[chip] for chip in some], axis=1)
+        part = weight_mine[:, start * depth : (start + step) * depth]
+        term = lax.dot_general(rows, part, NT, preferred_element_type=F32)
         total = term if total is None else total + term
     part_ref[...] = total
     for copy in small[2:] + other:
@@ -82,12 +87,10 @@
     group, other_ref, part_ref, weight_ref, gate_ref, conv_out_ref, conv_turned_ref, taps_ref,
     grad_gate_ref, out_ref, rows_ref,
 ):
-    chips, _, depth = other_ref.shape
+    chips = other_ref.shape[0]
     peers = rows_ref.shape[0] // IN_ROWS
-    dmix = part_ref[...]
-    for chip in range(chips):
-        part = weight_ref[:, chip * depth : (chip + 1) * depth]
-        dmix += lax.dot_general(other_ref[chip], part, NT, preferred_element_type=F32)
+    rows = jnp.concatenate([other_ref[chip] for chip in range(chips)], axis=1)
+    dmix = part_ref[...] + lax.dot_general(rows, weight_ref[...], NT, preferred_element_type=F32)
     grad_gate_ref[...] = (dmix * conv_out_ref[...].astype(F32)).astype(BF16)
     signal = upper(gate_ref[...].astype(F32) * dmix).T
     for j in range(group):
@@ -100,15 +103,18 @@
 
 def conv_body(
     group, blocks, skip_ref, place_ref, in_ref, out_ref,
-    in_rows, padded, shifted, toeplitz, out_rows,
+    in_rows, padded, moved_rows, spans, taps_spans, out_rows,
 ):
     peers = in_rows.shape[0] // IN_ROWS
+    parts = LANES // PART
     in_rows[...] = in_ref[...].astype(F32)
     row = lax.broadcasted_iota(jnp.int32, (LANES, LANES), 0)
     lane = lax.broadcasted_iota(jnp.int32, (LANES, LANES), 1)
     flip = (row + lane == LANES - 1).astype(BF16)
-    below = lane < row
-    keep = lane <= row
+    below = (lane < row)[:PART]
+    keep = (lane <= row + (LANES - PART))[:PART]
+    left = (lane < peers)[:PART]
+    rows_lane = lax.broadcasted_iota(jnp.int32, (peers + blocks, LANES), 1)
     tap_lane = lax.broadcasted_iota(jnp.int32, (blocks, LANES), 1) // (LANES // group)
     quarter = LANES // group
     place = place_ref[0]
@@ -117,42 +123,64 @@
         high = in_rows[pl.ds(part * IN_ROWS + group, blocks, stride=group * IN_ROWS), :]
         low = in_rows[pl.ds(part * IN_ROWS + group + 1, blocks, stride=group * IN_ROWS), :]
         tap_rows.append(high + low)
-    padded[peers:, :] = jnp.zeros((padded.shape[0] - peers, LANES), F32)
     lag_rows = []
     for j in range(group):
         signal = in_rows[pl.ds(group + 2 + j, peers, stride=IN_ROWS), :]
         conv = in_rows[pl.ds(j, peers, stride=IN_ROWS), :].astype(BF16)
-        padded[:peers, :] = signal
-        for k in range(blocks + 1):
-            shifted[:, k * LANES : (k + 1) * LANES] = padded[k : k + peers, :].astype(BF16)
+        padded[j, :peers, :] = signal
+        padded[j, peers:, :] = jnp.zeros((padded.shape[1] - peers, LANES), F32)
+        for a in range(parts):
+            if a > 0:
+                turned = pltpu.roll(padded[j], LANES - a * PART, 1)
+                moved_rows[j] = turned
+                here = moved_rows[j, : peers + blocks, :]
+                following = moved_rows[j, 1 : peers + blocks + 1, :]
+                padded_a = jnp.where(rows_lane < LANES - a * PART, here, following)
+                moved_rows[j, : peers + blocks, :] = padded_a
+            source = padded if a == 0 else moved_rows
+            for k in range(blocks + 1):
+                rows = source[j, k : k + peers, :].astype(BF16)
+                spans[j, a * peers : (a + 1) * peers, k * LANES : (k + 1) * LANES] = rows
         taps = jnp.zeros((blocks, LANES), F32)
         for part in range(group):
             moved = pltpu.roll(tap_rows[part], (part - j) % group * quarter, 1)
             taps = jnp.where(tap_lane == part, moved, taps)
-        before = jnp.zeros((LANES, LANES), F32)
+        before = jnp.zeros((PART, LANES), F32)
         for k in range(blocks + 1):
             if k < blocks:
-                spread = jnp.broadcast_to(taps[k : k + 1, :], (LANES, LANES))
+                spread = jnp.broadcast_to(taps[k : k + 1, :], (PART, LANES))
                 now = pltpu.roll(spread, 0, 1, stride=1, stride_axis=0)
             else:
-                now = jnp.zeros((LANES, LANES), F32)
+                now = jnp.zeros((PART, LANES), F32)
             both = jnp.where(below, before, now)
             high = both.astype(BF16)
-            toeplitz[:LANES, k * LANES : (k + 1) * LANES] = high
-            toeplitz[LANES:, k * LANES : (k + 1) * LANES] = (both - high.astype(F32)).astype(BF16)
+            taps_spans[j, :PART, k * LANES : (k + 1) * LANES] = high
+            taps_spans[j, PART:, k * LANES : (k + 1) * LANES] = (both - high.astype(F32)).astype(BF16)
             before = now
-        corr = lax.dot_general(toeplitz[...], shifted[...], NT, preferred_element_type=F32)
-        corr = (corr[:LANES] + corr[LANES:]).T
+        corr = lax.dot_general(taps_spans[j], spans[j], NT, preferred_element_type=F32)
+        corr = corr[:PART] + corr[PART:]
+        stacked = []
+        for a in range(0, parts, 2):
+            pair = corr[:, a * peers : (a + 2) * peers]
+            stacked += [pair, pltpu.roll(pair, peers, 1)]
+        corr = jnp.concatenate(stacked, axis=0).T[:peers]
         gain = skip_ref[j * peers + place]
         out_rows[pl.ds(j, peers, stride=OUT_ROWS), :] = corr + gain * signal
-        turned = lax.dot_general(flip, conv, NT, preferred_element_type=F32).astype(BF16)
-        products = jnp.dot(turned, shifted[...], preferred_element_type=F32)
+        twice = jnp.concatenate([conv, conv], axis=0)
+        turned = lax.dot_general(flip, twice, NT, preferred_element_type=F32)
+        pairs = []
+        for a in range(0, parts, 2):
+            even = turned[LANES - (a + 1) * PART : LANES - a * PART]
+            odd = turned[LANES - (a + 2) * PART : LANES - (a + 1) * PART]
+            pairs.append(jnp.where(left, even, odd).astype(BF16))
+        factors = pairs[0] if len(pairs) == 1 else jnp.concatenate(pairs, axis=1)
+        products = jnp.dot(factors, spans[j], preferred_element_type=F32)
         sums = []
-        now = pltpu.roll(products[:, :LANES], 1, 1, stride=1, stride_axis=0)
+        first = LANES + 1 - PART
+        now = pltpu.roll(products[:, :LANES], first, 1, stride=1, stride_axis=0)
         for k in range(blocks):
-            later = pltpu.roll(
-                products[:, (k + 1) * LANES : (k + 2) * LANES], 1, 1, stride=1, stride_axis=0
-            )
+            tile = products[:, (k + 1) * LANES : (k + 2) * LANES]
+            later = pltpu.roll(tile, first, 1, stride=1, stride_axis=0)
             sums.append(jnp.sum(jnp.where(keep, now, later), axis=0, keepdims=True))
             now = later
         lag_rows.append(jnp.concatenate(sums, axis=0))
@@ -202,6 +230,7 @@
 
     chips = lax.axis_size("ch") // 2
     core = (lax.axis_index("ch") % 2).astype(jnp.int32).reshape(1)
+    core, place = lax.optimization_barrier((core, place))
     sides = [[2 * chip + side for chip in range(chips)] for side in range(2)]
     copies = jnp.broadcast_to(grad_out[None], (chips, tok_rows, chan_width))
     mine = lax.all_to_all(copies, "ch", 0, 0, tiled=True, axis_index_groups=sides)
@@ -250,9 +279,10 @@
         shape((peers * OUT_ROWS, tok_rows), BF16),
         [
             vmem((peers * IN_ROWS, tok_rows), F32),
-            vmem((peers + blocks, tok_rows), F32),
-            vmem((peers, span), BF16),
-            vmem((2 * tok_rows, span), BF16),
+            vmem((group, peers + blocks + 8, tok_rows), F32),
+            vmem((group, peers + blocks + 8, tok_rows), F32),
+            vmem((group, peers * (tok_rows // PART), span), BF16),
+            vmem((group, 2 * PART, span), BF16),
             vmem((peers * OUT_ROWS, tok_rows), F32),
         ],
         6 * group * peers * tok_rows * span,

time: 98.1 us -> 95.8 us (0.977)
  blocking collectives: 44.5 us -> 85.1 us
  starting transfers between devices: 24.2 us -> 1.91 us
  waiting for transfers between devices: 18.5 us -> 0.01 us
  Pallas kernels: 8.95 us -> 6.85 us
    all_to_all x1 -> x2, blocking collectives: 20.1 us -> 60.7 us  [exchange(): return lax.all_to_all(pairs, 'ctx', 0, 0, tiled=True).reshape(rows.shape)]
    all_to_all x1 -> x0, starting transfers between devices: 22.3 us -> none  [exchange(): return lax.all_to_all(pairs, 'ctx', 0, 0, tiled=True).reshape(rows.shape)]
    all_to_all x1 -> x0, waiting for transfers between devices: 18.5 us -> none  [exchange(): return lax.all_to_all(pairs, 'ctx', 0, 0, tiled=True).reshape(rows.shape)]
    pallas_call x1, Pallas kernels: 4.2 us -> 2.66 us  [local(): call(functools.partial(conv_body, group, blocks), shape((peers * OUT_ROWS...]
  transfers between devices with their start and end apart: 2 -> 1, of which waited for: 1 -> 0; matrix products, arithmetic and copies ran while one was open for 0% -> 0% of each run, Pallas kernels for 3% -> 2%
where the time goes in v3:
time: 95.8 us; the launch traced here: 95.4 us
  blocking collectives  85.1 us (89%)
  Pallas kernels  6.85 us (7%)
  starting transfers between devices  1.91 us (2%)
    all_to_all x2, blocking collectives, exchange(): return lax.all_to_all(pairs, 'ctx', 0, 0, tiled=True).reshape(rows.shape)  60.7 us
    all_to_all x1, blocking collectives, local(): lax.all_to_all(copies, 'ch', 0, 0, tiled=True, axis_index_groups=sides)  24.4 us
    pallas_call x1, Pallas kernels, local(): call(functools.partial(conv_body, group, blocks), shape((peers * OUT_ROWS...  2.66 us
    pallas_call x1, Pallas kernels, local(): call(functools.partial(first_body, group), (shape(local_shape, F32), shap...  2.32 us
  transfers between devices with their start and end apart: 1, of which 0 were waited for; matrix products, arithmetic and copies ran while one was open for 0% of the time, Pallas kernels for 2%

profile of v3, /device:TPU:2, one launch (start us, length us, event | category | flops | bytes accessed | tf_op | source)
XLA Modules:
  0.0 95.4 jit_solution(2459661226092063183)
XLA Ops:
  0.6 0.9 broadcast_in_dim.2
  1.5 24.4 %all_to_all.15.mine_ref = bf16[8,128,256]{2,1,0:T(8,128)(2,1)S(1)} all-to-all(bf16[8,128,256]{2,1,0:T(8,128)(2,1)S(1)} %broadcast_in_dim.2), channel_id=1, replica_groups={{0,2,4,6,8,10,12,14},{1,3,5,7,9,11,13,15},{16,18,20,22,24,26,28,30},{17..., dimensions={0} | all-to-all | bytes 1048576 | tf_op jit(solution)/shard_map/all_to_all | solution.py:236
  25.9 1.9 %collective-permute-start = (bf16[8,128,256]{2,1,0:T(8,128)(2,1)S(1)}, bf16[8,128,256]{2,1,0:T(8,128)(2,1)S(1)}, u32[]{:S(2)}, u32[]{:S(2)}) collective-permute-start(bf16[8,128,256]{2,1,0:T(8,128)(2,1)S(1)} %all_to_all.15.mine_ref), channel_id=1, source_target_pairs={{0,1},{1,0},{2,3},{3,2},{4,5},{5,4},{6,7},{7,6},{8,9},{9,8},{10,11... | collective-permute-start | bytes 1572872 | tf_op jit(solution)/shard_map/ppermute | solution.py:237
  27.8 0.0 copy-start
  27.8 2.3 %shard_map.94 = (f32[128,256]{1,0:T(8,128)S(1)}, bf16[256,2048]{1,0:T(8,128)(2,1)S(1)}, bf16[128,256]{1,0:T(8,128)(2,1)S(1)}, bf16[128,256]{1,0:T(8,128)(2,1)S(1...) custom-call(s32[1]{0:T(128)} %bitcast.core_ref, bf16[8,128,256]{2,1,0:T(8,128)(2,1)S(1)} %all_to_all.15.mine_ref, ...), custom_call_target="tpu_custom_call" | custom-call | flops 134217728 | bytes 2097152 | tf_op jit(solution)/shard_map/pallas_call | solution.py:244
  30.2 0.0 collective-permute-done.other_ref
  30.2 1.1 %shard_map.95 = (bf16[128,256]{1,0:T(8,128)(2,1)}, bf16[640,128]{1,0:T(8,128)(2,1)S(1)}) custom-call(bf16[8,128,256]{2,1,0:T(8,128)(2,1)S(1)} %collective-permute-done.other_ref, f32[128,256]{1,0:T(8,128)S(1)} %get-tuple-element.17.part_ref, bf16[256,2048]{1,0:T(8,128)(2,1)S(1)} %get-tuple-element.18.weight_ref, ...), custom_call_target="tpu_custom_call" | custom-call | flops 134217728 | bytes 2097152 | tf_op jit(solution)/shard_map/pallas_call | solution.py:267
  31.3 40.6 %all_to_all.16 = bf16[64,5,2,128]{3,2,1,0:T(2,128)(2,1)S(1)} all-to-all(bf16[64,5,2,128]{3,2,1,0:T(2,128)(2,1)S(1)} %bitcast.7), channel_id=1, replica_groups=mesh['ctx'=64,'ch'=16] {'ctx'}, dimensions={0} | all-to-all | bytes 327680 | tf_op jit(solution)/shard_map/all_to_all | solution.py:216
  71.9 0.0 copy-done
  71.9 2.7 %shard_map.96 = bf16[384,128]{1,0:T(8,128)(2,1)S(1)} custom-call(f32[256]{0:T(256)S(1)} %copy-done, s32[1]{0:T(128)} %bitcast.1.place_ref, bf16[640,128]{1,0:T(8,128)(2,1)S(1)} %bitcast.8), custom_call_target="tpu_custom_call" | custom-call | flops 427819008 | bytes 1000000 | tf_op jit(solution)/shard_map/pallas_call | solution.py:277
  74.6 20.1 %all_to_all.17 = bf16[64,3,2,128]{3,2,1,0:T(2,128)(2,1)S(1)} all-to-all(bf16[64,3,2,128]{3,2,1,0:T(2,128)(2,1)S(1)} %bitcast.9), channel_id=1, replica_groups=mesh['ctx'=64,'ch'=16] {'ctx'}, dimensions={0} | all-to-all | bytes 196608 | tf_op jit(solution)/shard_map/all_to_all | solution.py:216
  94.7 0.8 shard_map.97
Async XLA Ops:
  25.9 4.3 %collective-permute-start = (bf16[8,128,256]{2,1,0:T(8,128)(2,1)S(1)}, bf16[8,128,256]{2,1,0:T(8,128)(2,1)S(1)}, u32[]{:S(2)}, u32[]{:S(2)}) collective-permute-start(bf16[8,128,256]{2,1,0:T(8,128)(2,1)S(1)} %all_to_all.15.mine_ref), channel_id=1, source_target_pairs={{0,1},{1,0},{2,3},{3,2},{4,5},{5,4},{6,7},{7,6},{8,9},{9,8},{10,11... | collective-permute-start | bytes 1572872 | tf_op jit(solution)/shard_map/ppermute | solution.py:237
  27.8 44.1 %copy-start = (f32[256]{0:T(256)S(1)}, f32[256]{0:T(256)}, u32[]{:S(2)}) copy-start(f32[256]{0:T(256)} %skip_ref.1) | copy-start | bytes 3076

commit v4 on v3

--- a/solution.py
+++ b/solution.py
@@ -33,9 +33,8 @@
 
 
 def first_body(
-    group, core_ref, mine_ref, weight_hbm, gate_hbm, conv_out_hbm, conv_hbm, taps_hbm,
-    part_ref, weight_ref, gate_ref, conv_out_ref, conv_turned_ref, taps_ref,
-    weight_mine, conv_here, taps_here, mine_sems, other_sems, sems,
+    group, core_ref, mine_ref, weight_hbm, conv_hbm, taps_hbm, part_ref, conv_turned_ref, taps_ref,
+    weight_mine, conv_here, taps_here, mine_sems, sems,
 ):
     chips, _, depth = mine_ref.shape
     peers = taps_ref.shape[1]
@@ -51,11 +50,8 @@
     small = [
         pltpu.make_async_copy(conv_hbm, conv_here, sems.at[0]),
         pltpu.make_async_copy(taps_hbm, taps_here, sems.at[1]),
-        pltpu.make_async_copy(gate_hbm, gate_ref, sems.at[2]),
-        pltpu.make_async_copy(conv_out_hbm, conv_out_ref, sems.at[3]),
     ]
-    other = [columns(1 - core, chip, weight_ref, other_sems) for chip in range(chips)]
-    for copy in small[:2] + mine + small[2:] + other:
+    for copy in small + mine:
         copy.start()
     small[0].wait()
     conv_turned_ref[...] = conv_here[...].astype(F32).T
@@ -79,18 +75,18 @@
         term = lax.dot_general(rows, part, NT, preferred_element_type=F32)
         total = term if total is None else total + term
     part_ref[...] = total
-    for copy in small[2:] + other:
-        copy.wait()
 
 
 def second_body(
-    group, other_ref, part_ref, weight_ref, gate_ref, conv_out_ref, conv_turned_ref, taps_ref,
+    group, core_ref, other_ref, part_ref, weight_ref, gate_ref, conv_out_ref, conv_turned_ref, taps_ref,
     grad_gate_ref, out_ref, rows_ref,
 ):
-    chips = other_ref.shape[0]
+    chips, _, depth = other_ref.shape
     peers = rows_ref.shape[0] // IN_ROWS
     rows = jnp.concatenate([other_ref[chip] for chip in range(chips)], axis=1)
-    dmix = part_ref[...] + lax.dot_general(rows, weight_ref[...], NT, preferred_element_type=F32)
+    starts = [pl.multiple_of((2 * chip + 1 - core_ref[0]) * depth, depth) for chip in range(chips)]
+    weight = jnp.concatenate([weight_ref[:, pl.ds(start, depth)] for start in starts], axis=1)
+    dmix = part_ref[...] + lax.dot_general(rows, weight, NT, preferred_element_type=F32)
     grad_gate_ref[...] = (dmix * conv_out_ref[...].astype(F32)).astype(BF16)
     signal = upper(gate_ref[...].astype(F32) * dmix).T
     for j in range(group):
@@ -103,7 +99,7 @@
 
 def conv_body(
     group, blocks, skip_ref, place_ref, in_ref, out_ref,
-    in_rows, padded, moved_rows, spans, taps_spans, out_rows,
+    in_rows, padded, moved_rows, spans, taps_spans, out_rows, table,
 ):
     peers = in_rows.shape[0] // IN_ROWS
     parts = LANES // PART
@@ -126,7 +122,6 @@
     lag_rows = []
     for j in range(group):
         signal = in_rows[pl.ds(group + 2 + j, peers, stride=IN_ROWS), :]
-        conv = in_rows[pl.ds(j, peers, stride=IN_ROWS), :].astype(BF16)
         padded[j, :peers, :] = signal
         padded[j, peers:, :] = jnp.zeros((padded.shape[1] - peers, LANES), F32)
         for a in range(parts):
@@ -157,6 +152,9 @@
             taps_spans[j, :PART, k * LANES : (k + 1) * LANES] = high
             taps_spans[j, PART:, k * LANES : (k + 1) * LANES] = (both - high.astype(F32)).astype(BF16)
             before = now
+    for j in range(group):
+        signal = padded[j, :peers, :]
+        conv = in_rows[pl.ds(j, peers, stride=IN_ROWS), :].astype(BF16)
         corr = lax.dot_general(taps_spans[j], spans[j], NT, preferred_element_type=F32)
         corr = corr[:PART] + corr[PART:]
         stacked = []
@@ -174,7 +172,9 @@
             odd = turned[LANES - (a + 2) * PART : LANES - (a + 1) * PART]
             pairs.append(jnp.where(left, even, odd).astype(BF16))
         factors = pairs[0] if len(pairs) == 1 else jnp.concatenate(pairs, axis=1)
-        products = jnp.dot(factors, spans[j], preferred_element_type=F32)
+        table[j] = jnp.dot(factors, spans[j], preferred_element_type=F32)
+    for j in range(group):
+        products = table.at[j]
         sums = []
         first = LANES + 1 - PART
         now = pltpu.roll(products[:, :LANES], first, 1, stride=1, stride_axis=0)
@@ -240,14 +240,11 @@
     dma = pltpu.SemaphoreType.DMA
     half = chips * chan_width
     local_shape = (tok_rows, chan_width)
-    stored = (out_weight, gate_values, conv_output, conv_input, long_filter)
-    ready = call(
+    stored = (out_weight, conv_input, long_filter)
+    part, conv_turned, taps = call(
         functools.partial(first_body, group),
         (
             shape(local_shape, F32),
-            shape((chan_width, half), BF16),
-            shape(local_shape, BF16),
-            shape(local_shape, BF16),
             shape((chan_width, tok_rows), F32),
             shape((2, peers, tok_rows), F32),
         ),
@@ -256,12 +253,11 @@
             vmem(local_shape, BF16),
             vmem((lag_rows, chan_width), F32),
             dma((chips,)),
-            dma((chips,)),
-            dma((4,)),
+            dma((2,)),
         ],
         tok_rows * out_weight.size,
         2 * out_weight.size,
-    )(in_specs=[smem, whole] + [hbm] * 5)(
+    )(in_specs=[smem, whole] + [hbm] * 3)(
         core, mine, *(pltpu.with_memory_space_constraint(held, pltpu.HBM) for held in stored)
     )
     grad_gate, rows = call(
@@ -270,7 +266,7 @@
         [vmem((peers * IN_ROWS, tok_rows), F32)],
         tok_rows * out_weight.size,
         2 * out_weight.size,
-    )()(other, *ready)
+    )(in_specs=[smem] + [whole] * 7)(core, other, part, out_weight, gate_values, conv_output, conv_turned, taps)
     rows = exchange(rows, IN_ROWS)
 
     span = (blocks + 1) * tok_rows
@@ -284,6 +280,7 @@
             vmem((group, peers * (tok_rows // PART), span), BF16),
             vmem((group, 2 * PART, span), BF16),
             vmem((peers * OUT_ROWS, tok_rows), F32),
+            vmem((group, PART, span), F32),
         ],
         6 * group * peers * tok_rows * span,
         1_000_000,

time: 95.8 us -> 95.6 us (level)
  no operation moved by 1% of the time
where the time goes in v4:
time: 95.6 us; the launch traced here: 95.3 us
  blocking collectives  85.1 us (89%)
  Pallas kernels  6.51 us (7%)
  starting transfers between devices  1.91 us (2%)
  local copies, waits for them, and re-layouts  1.05 us (1%)
    all_to_all x2, blocking collectives, exchange(): return lax.all_to_all(pairs, 'ctx', 0, 0, tiled=True).reshape(rows.shape)  60.7 us
    all_to_all x1, blocking collectives, local(): lax.all_to_all(copies, 'ch', 0, 0, tiled=True, axis_index_groups=sides)  24.4 us
    pallas_call x1, Pallas kernels, local(): call(functools.partial(conv_body, group, blocks), shape((peers * OUT_ROWS...  2.56 us
    pallas_call x1, Pallas kernels, local(): call(functools.partial(first_body, group), (shape(local_shape, F32), shap...  2.06 us
  transfers between devices with their start and end apart: 1, of which 0 were waited for; matrix products, arithmetic and copies ran while one was open for 0% of the time, Pallas kernels for 2%

profile of v4, /device:TPU:2, one launch (start us, length us, event | category | flops | bytes accessed | tf_op | source)
XLA Modules:
  0.0 95.3 jit_solution(7630941162687434179)
XLA Ops:
  0.6 0.0 copy-start
  0.6 0.0 copy-start.1
  0.7 0.0 copy-start.2
  0.7 1.0 %broadcast_in_dim.2 = bf16[8,128,256]{2,1,0:T(8,128)(2,1)S(1)} broadcast(bf16[128,256]{1,0:T(8,128)(2,1)} %param.7), dimensions={1,2} | broadcast | bytes 589824 | tf_op jit(solution)/shard_map/broadcast_in_dim | solution.py:235
  1.7 24.4 %all_to_all.15.mine_ref = bf16[8,128,256]{2,1,0:T(8,128)(2,1)S(1)} all-to-all(bf16[8,128,256]{2,1,0:T(8,128)(2,1)S(1)} %broadcast_in_dim.2), channel_id=1, replica_groups={{0,2,4,6,8,10,12,14},{1,3,5,7,9,11,13,15},{16,18,20,22,24,26,28,30},{17..., dimensions={0} | all-to-all | bytes 1048576 | tf_op jit(solution)/shard_map/all_to_all | solution.py:236
  26.1 1.9 %collective-permute-start = (bf16[8,128,256]{2,1,0:T(8,128)(2,1)S(1)}, bf16[8,128,256]{2,1,0:T(8,128)(2,1)S(1)}, u32[]{:S(2)}, u32[]{:S(2)}) collective-permute-start(bf16[8,128,256]{2,1,0:T(8,128)(2,1)S(1)} %all_to_all.15.mine_ref), channel_id=1, source_target_pairs={{0,1},{1,0},{2,3},{3,2},{4,5},{5,4},{6,7},{7,6},{8,9},{9,8},{10,11... | collective-permute-start | bytes 1572872 | tf_op jit(solution)/shard_map/ppermute | solution.py:237
  28.0 2.1 %shard_map.94 = (f32[128,256]{1,0:T(8,128)S(1)}, f32[256,128]{1,0:T(8,128)S(1)}, f32[2,64,128]{2,1,0:T(8,128)S(1)}) custom-call(s32[1]{0:T(128)} %bitcast.core_ref, bf16[8,128,256]{2,1,0:T(8,128)(2,1)S(1)} %all_to_all.15.mine_ref, bf16[256,4096]{1,0:T(8,128)(2,1)} %weight_ref.1, bf16[128,256]{1,0:T(8,128)(2,1)} %conv_hbm.1, f32[32,256]{1,0:T(8,128)} %taps_hbm.1), custom_call_target="tpu_custom_call" | custom-call | flops 134217728 | bytes 2097152 | tf_op jit(solution)/shard_map/pallas_call | solution.py:244
  30.1 0.0 copy-start.3
  30.1 0.0 collective-permute-done.other_ref
  30.1 0.0 copy-done
  30.1 0.0 copy-done.1
  30.1 0.0 copy-done.2
  30.1 1.1 %shard_map.95 = (bf16[128,256]{1,0:T(8,128)(2,1)}, bf16[640,128]{1,0:T(8,128)(2,1)S(1)}) custom-call(s32[1]{0:T(128)} %bitcast.core_ref, bf16[8,128,256]{2,1,0:T(8,128)(2,1)S(1)} %collective-permute-done.other_ref, f32[128,256]{1,0:T(8,128)S(1)} %get-tuple-element.14.part_ref, bf16[256,4096]{1,0:T(8,128)(2,1)S(1)} %copy-done, ...), custom_call_target="tpu_custom_call" | custom-call | flops 134217728 | bytes 2097152 | tf_op jit(solution)/shard_map/pallas_call | solution.py:263
  31.3 40.6 %all_to_all.16 = bf16[64,5,2,128]{3,2,1,0:T(2,128)(2,1)S(1)} all-to-all(bf16[64,5,2,128]{3,2,1,0:T(2,128)(2,1)S(1)} %bitcast.7), channel_id=1, replica_groups=mesh['ctx'=64,'ch'=16] {'ctx'}, dimensions={0} | all-to-all | bytes 327680 | tf_op jit(solution)/shard_map/all_to_all | solution.py:216
  71.9 0.0 copy-done.3
  71.9 2.6 %shard_map.96 = bf16[384,128]{1,0:T(8,128)(2,1)S(1)} custom-call(f32[256]{0:T(256)S(1)} %copy-done.3, s32[1]{0:T(128)} %bitcast.1.place_ref, bf16[640,128]{1,0:T(8,128)(2,1)S(1)} %bitcast.8), custom_call_target="tpu_custom_call" | custom-call | flops 427819008 | bytes 1000000 | tf_op jit(solution)/shard_map/pallas_call | solution.py:273
  74.5 20.1 %all_to_all.17 = bf16[64,3,2,128]{3,2,1,0:T(2,128)(2,1)S(1)} all-to-all(bf16[64,3,2,128]{3,2,1,0:T(2,128)(2,1)S(1)} %bitcast.9), channel_id=1, replica_groups=mesh['ctx'=64,'ch'=16] {'ctx'}, dimensions={0} | all-to-all | bytes 196608 | tf_op jit(solution)/shard_map/all_to_all | solution.py:216
  94.6 0.8 shard_map.97
Async XLA Ops:
  0.6 29.5 %copy-start = (bf16[256,4096]{1,0:T(8,128)(2,1)S(1)}, bf16[256,4096]{1,0:T(8,128)(2,1)}, u32[]{:S(2)}) copy-start(bf16[256,4096]{1,0:T(8,128)(2,1)} %weight_ref.1) | copy-start | bytes 6291460
  0.6 29.5 %copy-start.1 = (bf16[128,256]{1,0:T(8,128)(2,1)S(1)}, bf16[128,256]{1,0:T(8,128)(2,1)}, u32[]{:S(2)}) copy-start(bf16[128,256]{1,0:T(8,128)(2,1)} %gate_ref.1) | copy-start | bytes 196612
  0.7 29.5 %copy-start.2 = (bf16[128,256]{1,0:T(8,128)(2,1)S(1)}, bf16[128,256]{1,0:T(8,128)(2,1)}, u32[]{:S(2)}) copy-start(bf16[128,256]{1,0:T(8,128)(2,1)} %conv_out_ref.1) | copy-start | bytes 196612
  26.1 4.0 %collective-permute-start = (bf16[8,128,256]{2,1,0:T(8,128)(2,1)S(1)}, bf16[8,128,256]{2,1,0:T(8,128)(2,1)S(1)}, u32[]{:S(2)}, u32[]{:S(2)}) collective-permute-start(bf16[8,128,256]{2,1,0:T(8,128)(2,1)S(1)} %all_to_all.15.mine_ref), channel_id=1, source_target_pairs={{0,1},{1,0},{2,3},{3,2},{4,5},{5,4},{6,7},{7,6},{8,9},{9,8},{10,11... | collective-permute-start | bytes 1572872 | tf_op jit(solution)/shard_map/ppermute | solution.py:237
  30.1 41.8 %copy-start.3 = (f32[256]{0:T(256)S(1)}, f32[256]{0:T(256)}, u32[]{:S(2)}) copy-start(f32[256]{0:T(256)} %skip_ref.1) | copy-start | bytes 3076

commit v5 on v4

--- a/solution.py
+++ b/solution.py
@@ -78,8 +78,8 @@
 
 
 def second_body(
-    group, core_ref, other_ref, part_ref, weight_ref, gate_ref, conv_out_ref, conv_turned_ref, taps_ref,
-    grad_gate_ref, out_ref, rows_ref,
+    group, core_ref, other_ref, part_ref, weight_ref, gate_ref, conv_turned_ref, taps_ref,
+    dmix_ref, out_ref, rows_ref,
 ):
     chips, _, depth = other_ref.shape
     peers = rows_ref.shape[0] // IN_ROWS
@@ -87,7 +87,7 @@
     starts = [pl.multiple_of((2 * chip + 1 - core_ref[0]) * depth, depth) for chip in range(chips)]
     weight = jnp.concatenate([weight_ref[:, pl.ds(start, depth)] for start in starts], axis=1)
     dmix = part_ref[...] + lax.dot_general(rows, weight, NT, preferred_element_type=F32)
-    grad_gate_ref[...] = (dmix * conv_out_ref[...].astype(F32)).astype(BF16)
+    dmix_ref[...] = dmix
     signal = upper(gate_ref[...].astype(F32) * dmix).T
     for j in range(group):
         rows_ref[pl.ds(j, peers, stride=IN_ROWS), :] = conv_turned_ref[j * peers : (j + 1) * peers]
@@ -260,14 +260,15 @@
     )(in_specs=[smem, whole] + [hbm] * 3)(
         core, mine, *(pltpu.with_memory_space_constraint(held, pltpu.HBM) for held in stored)
     )
-    grad_gate, rows = call(
+    dmix, rows = call(
         functools.partial(second_body, group),
-        (shape(local_shape, BF16), shape((peers * IN_ROWS, tok_rows), BF16)),
+        (shape(local_shape, F32), shape((peers * IN_ROWS, tok_rows), BF16)),
         [vmem((peers * IN_ROWS, tok_rows), F32)],
         tok_rows * out_weight.size,
         2 * out_weight.size,
-    )(in_specs=[smem] + [whole] * 7)(core, other, part, out_weight, gate_values, conv_output, conv_turned, taps)
+    )(in_specs=[smem] + [whole] * 6)(core, other, part, out_weight, gate_values, conv_turned, taps)
     rows = exchange(rows, IN_ROWS)
+    grad_gate = (dmix * conv_output.astype(F32)).astype(BF16)
 
     span = (blocks + 1) * tok_rows
     back = call(

time: 95.6 us -> 96.1 us (level)
  blocking collectives: 85.1 us -> 65.1 us
  waiting for transfers between devices: 0.01 us -> 14.3 us
  starting transfers between devices: 1.91 us -> 7.43 us
    all_to_all x2 -> x1, blocking collectives: 60.7 us -> 40.7 us  [exchange(): return lax.all_to_all(pairs, 'ctx', 0, 0, tiled=True).reshape(rows.shape)]
    all_to_all x0 -> x1, waiting for transfers between devices: none -> 14.3 us  [exchange(): return lax.all_to_all(pairs, 'ctx', 0, 0, tiled=True).reshape(rows.shape)]
    all_to_all x0 -> x1, starting transfers between devices: none -> 5.52 us  [exchange(): return lax.all_to_all(pairs, 'ctx', 0, 0, tiled=True).reshape(rows.shape)]
  transfers between devices with their start and end apart: 1 -> 2, of which waited for: 0 -> 1; matrix products, arithmetic and copies ran while one was open for 0% -> 1% of each run, Pallas kernels for 2% -> 2%
where the time goes in v5:
time: 96.1 us; the launch traced here: 95.8 us
  blocking collectives  65.1 us (68%)
  waiting for transfers between devices  14.3 us (15%)
  starting transfers between devices  7.43 us (8%)
  Pallas kernels  6.6 us (7%)
  local copies, waits for them, and re-layouts  1.05 us (1%)
    all_to_all x1, blocking collectives, exchange(): return lax.all_to_all(pairs, 'ctx', 0, 0, tiled=True).reshape(rows.shape)  40.7 us
    all_to_all x1, blocking collectives, local(): lax.all_to_all(copies, 'ch', 0, 0, tiled=True, axis_index_groups=sides)  24.4 us
    all_to_all x1, waiting for transfers between devices, exchange(): return lax.all_to_all(pairs, 'ctx', 0, 0, tiled=True).reshape(rows.shape)  14.3 us
    all_to_all x1, starting transfers between devices, exchange(): return lax.all_to_all(pairs, 'ctx', 0, 0, tiled=True).reshape(rows.shape)  5.52 us
    pallas_call x1, Pallas kernels, local(): call(functools.partial(conv_body, group, blocks), shape((peers * OUT_ROWS...  3.2 us
    pallas_call x1, Pallas kernels, local(): call(functools.partial(first_body, group), (shape(local_shape, F32), shap...  2.06 us
  transfers between devices with their start and end apart: 2, of which 1 were waited for; matrix products, arithmetic and copies ran while one was open for 1% of the time, Pallas kernels for 2%

profile of v5, /device:TPU:2, one launch (start us, length us, event | category | flops | bytes accessed | tf_op | source)
XLA Modules:
  0.0 95.8 jit_solution(3110929470094010363)
XLA Ops:
  0.6 0.0 copy-start
  0.6 0.0 copy-start.1
  0.7 1.0 %broadcast_in_dim.2 = bf16[8,128,256]{2,1,0:T(8,128)(2,1)S(1)} broadcast(bf16[128,256]{1,0:T(8,128)(2,1)} %param.7), dimensions={1,2} | broadcast | bytes 589824 | tf_op jit(solution)/shard_map/broadcast_in_dim | solution.py:235
  1.7 24.4 %all_to_all.15.mine_ref = bf16[8,128,256]{2,1,0:T(8,128)(2,1)S(1)} all-to-all(bf16[8,128,256]{2,1,0:T(8,128)(2,1)S(1)} %broadcast_in_dim.2), channel_id=1, replica_groups={{0,2,4,6,8,10,12,14},{1,3,5,7,9,11,13,15},{16,18,20,22,24,26,28,30},{17..., dimensions={0} | all-to-all | bytes 1048576 | tf_op jit(solution)/shard_map/all_to_all | solution.py:236
  26.1 1.9 %collective-permute-start = (bf16[8,128,256]{2,1,0:T(8,128)(2,1)S(1)}, bf16[8,128,256]{2,1,0:T(8,128)(2,1)S(1)}, u32[]{:S(2)}, u32[]{:S(2)}) collective-permute-start(bf16[8,128,256]{2,1,0:T(8,128)(2,1)S(1)} %all_to_all.15.mine_ref), channel_id=1, source_target_pairs={{0,1},{1,0},{2,3},{3,2},{4,5},{5,4},{6,7},{7,6},{8,9},{9,8},{10,11... | collective-permute-start | bytes 1572872 | tf_op jit(solution)/shard_map/ppermute | solution.py:237
  28.0 2.1 %shard_map.94 = (f32[128,256]{1,0:T(8,128)S(1)}, f32[256,128]{1,0:T(8,128)S(1)}, f32[2,64,128]{2,1,0:T(8,128)S(1)}) custom-call(s32[1]{0:T(128)} %bitcast.core_ref, bf16[8,128,256]{2,1,0:T(8,128)(2,1)S(1)} %all_to_all.15.mine_ref, bf16[256,4096]{1,0:T(8,128)(2,1)} %weight_ref.1, bf16[128,256]{1,0:T(8,128)(2,1)} %conv_hbm.1, f32[32,256]{1,0:T(8,128)} %taps_hbm.1), custom_call_target="tpu_custom_call" | custom-call | flops 134217728 | bytes 2097152 | tf_op jit(solution)/shard_map/pallas_call | solution.py:244
  30.1 0.0 copy-start.2
  30.1 0.0 collective-permute-done.other_ref
  30.1 0.0 copy-done
  30.1 0.0 copy-done.1
  30.1 0.0 copy-start.3
  30.1 0.6 shard_map.95
  30.7 40.7 %all_to_all.16 = bf16[64,5,2,128]{3,2,1,0:T(2,128)(2,1)S(1)} all-to-all(bf16[64,5,2,128]{3,2,1,0:T(2,128)(2,1)S(1)} %bitcast.7), channel_id=1, replica_groups=mesh['ctx'=64,'ch'=16] {'ctx'}, dimensions={0} | all-to-all | bytes 327680 | tf_op jit(solution)/shard_map/all_to_all | solution.py:216
  71.4 0.0 copy-done.2
  71.4 3.2 %shard_map.96 = bf16[384,128]{1,0:T(8,128)(2,1)} custom-call(f32[256]{0:T(256)S(1)} %copy-done.2, s32[1]{0:T(128)} %bitcast.1.place_ref, bf16[640,128]{1,0:T(8,128)(2,1)S(1)} %bitcast.8), custom_call_target="tpu_custom_call" | custom-call | flops 427819008 | bytes 1000000 | tf_op jit(solution)/shard_map/pallas_call | solution.py:274
  74.6 5.5 %all-to-all-start.2 = ((bf16[64,3,2,128]{3,2,1,0:T(2,128)(2,1)}), bf16[64,3,2,128]{3,2,1,0:T(2,128)(2,1)S(1)}, u32[]{:S(2)}, u32[]{:S(2)}) async-start(bf16[64,3,2,128]{3,2,1,0:T(2,128)(2,1)} %bitcast.4), calls=%async_computation.2 | async-start | bytes 196608 | tf_op jit(solution)/shard_map/all_to_all | solution.py:216
  80.1 0.0 copy-done.3
  80.1 0.6 multiply_convert_fusion
  80.8 14.3 %all-to-all-done.2 = bf16[64,3,2,128]{3,2,1,0:T(2,128)(2,1)S(1)} async-done(((bf16[64,3,2,128]{3,2,1,0:T(2,128)(2,1)}), bf16[64,3,2,128]{3,2,1,0:T(2,128)(2,1)S(1)}, u32[]{:S(2)}, u32[]{:S(2)}) %all-to-all-start.2) | async-done | bytes 98336 | tf_op jit(solution)/shard_map/all_to_all | solution.py:216
  95.0 0.8 shard_map.97
Async XLA Ops:
  0.6 29.5 %copy-start = (bf16[256,4096]{1,0:T(8,128)(2,1)S(1)}, bf16[256,4096]{1,0:T(8,128)(2,1)}, u32[]{:S(2)}) copy-start(bf16[256,4096]{1,0:T(8,128)(2,1)} %weight_ref.1) | copy-start | bytes 6291460
  0.6 29.5 %copy-start.1 = (bf16[128,256]{1,0:T(8,128)(2,1)S(1)}, bf16[128,256]{1,0:T(8,128)(2,1)}, u32[]{:S(2)}) copy-start(bf16[128,256]{1,0:T(8,128)(2,1)} %gate_ref.1) | copy-start | bytes 196612
  26.1 4.0 %collective-permute-start = (bf16[8,128,256]{2,1,0:T(8,128)(2,1)S(1)}, bf16[8,128,256]{2,1,0:T(8,128)(2,1)S(1)}, u32[]{:S(2)}, u32[]{:S(2)}) collective-permute-start(bf16[8,128,256]{2,1,0:T(8,128)(2,1)S(1)} %all_to_all.15.mine_ref), channel_id=1, source_target_pairs={{0,1},{1,0},{2,3},{3,2},{4,5},{5,4},{6,7},{7,6},{8,9},{9,8},{10,11... | collective-permute-start | bytes 1572872 | tf_op jit(solution)/shard_map/ppermute | solution.py:237
  30.1 41.3 %copy-start.2 = (f32[256]{0:T(256)S(1)}, f32[256]{0:T(256)}, u32[]{:S(2)}) copy-start(f32[256]{0:T(256)} %skip_ref.1) | copy-start | bytes 3076
  30.1 50.0 %copy-start.3 = (bf16[128,256]{1,0:T(8,128)(2,1)S(1)}, bf16[128,256]{1,0:T(8,128)(2,1)}, u32[]{:S(2)}) copy-start(bf16[128,256]{1,0:T(8,128)(2,1)} %param.11) | copy-start | bytes 196612
  74.6 20.5 %all-to-all-start.2 = ((bf16[64,3,2,128]{3,2,1,0:T(2,128)(2,1)}), bf16[64,3,2,128]{3,2,1,0:T(2,128)(2,1)S(1)}, u32[]{:S(2)}, u32[]{:S(2)}) async-start(bf16[64,3,2,128]{3,2,1,0:T(2,128)(2,1)} %bitcast.4), calls=%async_computation.2 | async-start | bytes 196608 | tf_op jit(solution)/shard_map/all_to_all | solution.py:216
